TPU v7x, 256 devices: a whole 4x4x8 slice. The times are simulated.
256 devices in a mesh: sec: 8 (over y, core), tile: 32 (over z, x).
Axes of the slice: x: 4, y: 4, z: 8, core: 2. Of those that a mesh axis runs over, the one named last changes fastest.
Arguments:
- tile_strips: bfloat16 [8, 32, 2, 5, 64, 512], P('sec', 'tile'), may hold values from -6 to 6, as said below
- pair_mask: int32 [8, 32, 2, 3], P('sec', 'tile'), may hold values 0 or 1
- strip_offset: int32 [8, 32, 2, 3, 2], P('sec', 'tile'), may hold values from -16 to 16
- stiffness: float32 [8, 32, 2], P('sec', 'tile'), may hold values from 0.05 to 0.5
Outputs:
- affine_update: float32 [6, 8, 32, 2], P(None, 'sec', 'tile')
- residual: float32 [6, 8, 32, 2], P(None, 'sec', 'tile')
Inputs may be any that keep to these rules, and one draw needn't show every extreme that they name: `tile_strips`: neighbouring tiles' intersecting images are correlated.
All inputs are finite; a program needn't handle non-finite values. No bound on the sum of `pair_mask` on one device may be relied on, other than what follows from the above.
Results may differ from a plain program's by a relative error of at most 0.0013.
Values may be sent and summed in bfloat16 or wider, within the bound.
No kernel may reach another device: no remote copies, remote signals or barrier semaphores. Data moves between devices by JAX's collectives and lax.ppermute only.
A program may use at most 64 MiB of HBM per device.

v0:
```python
import jax
import jax.numpy as jnp
from jax import lax
from jax.sharding import PartitionSpec as P

ITERS = 3


highest = lax.Precision.HIGHEST


def passed_along(shard, axis, by):
    length = lax.axis_size(axis)
    pairs = [(i, i + by) for i in range(length) if 0 <= i + by < length]
    return lax.ppermute(shard, axis, pairs)


def with_halo(cells, sides, width):
    for axis, dim in sides:
        count = lax.axis_size(axis)
        ends = count - 1
        head = lax.slice_in_dim(cells, 0, width, axis=dim)
        tail = lax.slice_in_dim(cells, cells.shape[dim] - width, cells.shape[dim], axis=dim)
        cells = jnp.concatenate(
            [
                lax.ppermute(tail, axis, [(i, (i + 1) % count) for i in range(ends)]),
                cells,
                lax.ppermute(head, axis, [((i + 1) % count, i) for i in range(ends)]),
            ],
            axis=dim,
        )
    return cells


def strip_gradients(image):
    padded = jnp.pad(image, 1)
    along_x = (padded[1:-1, 2:] - padded[1:-1, :-2]) * 0.5
    along_y = (padded[2:, 1:-1] - padded[:-2, 1:-1]) * 0.5
    return (along_x, along_y)


def jacobian_rows(image, shift_x, shift_y):
    height, width = image.shape
    column_grid = jnp.arange(width, dtype=jnp.float32)[None, :]
    row_grid = jnp.arange(height, dtype=jnp.float32)[:, None]
    coord_u = (column_grid + shift_x) / width - 0.5
    coord_v = (row_grid + shift_y) / height - 0.5
    along_x, along_y = strip_gradients(image)
    stacked = jnp.stack(
        [
            along_x * coord_u,
            along_x * coord_v,
            along_x,
            along_y * coord_u,
            along_y * coord_v,
            along_y,
        ]
    )
    return stacked.reshape(6, height * width)


def pair_block(image_a, image_b, offset):
    first = image_a.astype(jnp.float32)
    second = image_b.astype(jnp.float32)
    shifts = offset.astype(jnp.float32)
    zero = jnp.zeros((), jnp.float32)
    jacobian = jnp.concatenate(
        [jacobian_rows(first, zero, zero), -jacobian_rows(second, shifts[0], shifts[1])], axis=0
    )
    pixels = first.shape[0] * first.shape[1]
    misfit = (first - second).reshape(pixels)
    normal = (
        jnp.dot(jacobian, jacobian.T, precision=highest, preferred_element_type=jnp.float32)
        / pixels
    )
    pull = (
        -jnp.dot(jacobian, misfit, precision=highest, preferred_element_type=jnp.float32) / pixels
    )
    return (normal, pull)


def to_next(array, axis):
    lead = jnp.zeros_like(lax.slice_in_dim(array, 0, 1, axis=axis))
    return jnp.concatenate(
        [lead, lax.slice_in_dim(array, 0, array.shape[axis] - 1, axis=axis)], axis=axis
    )


def from_next(array, axis):
    tail = jnp.zeros_like(lax.slice_in_dim(array, 0, 1, axis=axis))
    return jnp.concatenate(
        [lax.slice_in_dim(array, 1, array.shape[axis], axis=axis), tail], axis=axis
    )


def apply_block(block, vector):
    return jnp.einsum("ij...,j...->i...", block, vector, precision=highest)


def cholesky_rows(matrix):
    order = matrix.shape[0]
    factor = [[None] * order for index in range(order)]
    for column in range(order):
        pivot = matrix[column, column]
        for inner in range(column):
            pivot = pivot - factor[column][inner] * factor[column][inner]
        pivot = jnp.sqrt(pivot)
        factor[column][column] = pivot
        for row in range(column + 1, order):
            entry = matrix[row, column]
            for inner in range(column):
                entry = entry - factor[row][inner] * factor[column][inner]
            factor[row][column] = entry / pivot
    return factor


def solve_rows(factor, vector):
    order = len(factor)
    forward = []
    for row in range(order):
        value = vector[row]
        for inner in range(row):
            value = value - factor[row][inner] * forward[inner]
        forward.append(value / factor[row][row])
    backward = [None] * order
    for row in reversed(range(order)):
        value = forward[row]
        for inner in range(row + 1, order):
            value = value - factor[inner][row] * backward[inner]
        backward[row] = value / factor[row][row]
    return jnp.stack(backward)


def tile_blocks(images_a, images_b, offsets, exists):
    normal, pull = lax.map(
        lambda items: pair_block(items[0], items[1], items[2]), (images_a, images_b, offsets)
    )
    return (jnp.transpose(normal, (1, 2, 0)) * exists, jnp.transpose(pull, (1, 0)) * exists)


def squares_sum(residual, scaled):
    return lax.psum(jnp.sum(residual * scaled), ("sec", "tile"))


def shards(tile_strips, pair_mask, strip_offset, stiffness):
    columns = tile_strips.shape[2]
    sections = lax.axis_size("sec")
    tile_rows = lax.axis_size("tile")
    section = lax.axis_index("sec")
    tile_row = lax.axis_index("tile")
    strips = tile_strips[0, 0]
    masks = pair_mask[0, 0]
    offsets = strip_offset[0, 0]
    column_index = jnp.arange(columns)
    exists_right = ((masks[:, 0] == 1) & (column_index < columns - 1)).astype(jnp.float32)
    exists_down = ((masks[:, 1] == 1) & (tile_row < tile_rows - 1)).astype(jnp.float32)
    exists_cross = ((masks[:, 2] == 1) & (section < sections - 1)).astype(jnp.float32)
    normal_right, pull_right = tile_blocks(
        strips[:, 1], from_next(strips[:, 0], 0), offsets[:, 0], exists_right
    )
    lower_top = passed_along(strips[:, 2], "tile", -1)
    normal_down, pull_down = tile_blocks(strips[:, 3], lower_top, offsets[:, 1], exists_down)
    later_patch = passed_along(strips[:, 4], "sec", -1)
    normal_cross, pull_cross = tile_blocks(strips[:, 4], later_patch, offsets[:, 2], exists_cross)
    upper_down = passed_along((normal_down[6:, 6:], normal_down[:6, 6:], pull_down[6:]), "tile", 1)
    upper_cross = passed_along(
        (normal_cross[6:, 6:], normal_cross[:6, 6:], pull_cross[6:]), "sec", 1
    )
    identity = jnp.eye(6, dtype=jnp.float32)[:, :, None]
    diagonal = (
        stiffness[0, 0][None, None, :] * identity
        + normal_right[:6, :6]
        + to_next(normal_right[6:, 6:], 2)
    )
    diagonal = diagonal + normal_down[:6, :6] + upper_down[0]
    diagonal = diagonal + normal_cross[:6, :6] + upper_cross[0]
    load = pull_right[:6] + to_next(pull_right[6:], 1) + pull_down[:6] + upper_down[2]
    load = load + pull_cross[:6] + upper_cross[2]
    coupling_right = normal_right[:6, 6:]
    coupling_down = normal_down[:6, 6:]
    coupling_cross = normal_cross[:6, 6:]
    factor = cholesky_rows(diagonal)
    affine_update = jnp.zeros_like(load)
    residual = load
    scaled = solve_rows(factor, residual)
    direction = scaled
    rho_now = squares_sum(residual, scaled)
    for step in range(ITERS):
        spread = with_halo(direction[:, None, None, :], (("sec", 1), ("tile", 2)), 1)
        result = apply_block(diagonal, direction)
        result = result + apply_block(coupling_right, from_next(direction, 1))
        result = result + to_next(apply_block(jnp.swapaxes(coupling_right, 0, 1), direction), 1)
        result = result + apply_block(coupling_down, spread[:, 1, 2])
        result = result + apply_block(jnp.swapaxes(upper_down[1], 0, 1), spread[:, 1, 0])
        result = result + apply_block(coupling_cross, spread[:, 2, 1])
        result = result + apply_block(jnp.swapaxes(upper_cross[1], 0, 1), spread[:, 0, 1])
        step_size = rho_now / lax.psum(jnp.sum(direction * result), ("sec", "tile"))
        affine_update = affine_update + step_size * direction
        residual = residual - step_size * result
        scaled = solve_rows(factor, residual)
        rho_next = squares_sum(residual, scaled)
        direction = scaled + rho_next / rho_now * direction
        rho_now = rho_next
    return (affine_update.reshape(6, 1, 1, columns), residual.reshape(6, 1, 1, columns))


def solution(mesh):
    return jax.shard_map(
        shards,
        mesh=mesh,
        in_specs=(
            P("sec", "tile", None, None, None, None),
            P("sec", "tile", None, None),
            P("sec", "tile", None, None, None),
            P("sec", "tile", None),
        ),
        out_specs=(P(None, "sec", "tile", None), P(None, "sec", "tile", None)),
        check_vma=False,
    )
```

profile of v0, /device:TPU:1, one launch (start us, length us, event | category | flops | bytes accessed | tf_op | source)
XLA Modules:
  0.0 618.1 jit_solution(1666930053040462030)
XLA Ops:
  3.9 5.1 collective-permute-start.2
  11.8 41.4 %while.45 = (s32[]{:T(128)}, f32[2,12,12]{2,1,0:T(8,128)S(1)}, f32[2,12]{1,0:T(2,128)}, bf16[2,64,512]{2,1,0:T(8,128)(2,1)}, bf16[2,64,512]{2,1,0:T(8,128)(2,1)}, /*index=5*/s32[2,2]{1,0:T(2,128)}, s32[]{:T(128)}, s32[]{:T(128)}) while((s32[]{:T(128)}, f32[2,12,12]{2,1,0:T(8,128)S(1)}, f32[2,12]{1,0:T(2,128)}, bf16[2,64,512]{2,1,0:T(8,128)(2,1)}, ...), condition=%wide.region_1.2_spmd, body=%wide.region_0.1_spmd.sunk | while | flops 62232948 | bytes 19164288 | solution.py:135
  22.5 3.9 concatenate.148
  29.0 2.8 fusion.151
  43.1 3.9 concatenate.148
  49.6 2.9 fusion.151
  59.3 42.7 %while.46 = (s32[]{:T(128)}, f32[2,12,12]{2,1,0:T(8,128)}, f32[2,12]{1,0:T(2,128)}, bf16[2,64,512]{2,1,0:T(8,128)(2,1)}, bf16[2,64,512]{2,1,0:T(8,128)(2,1)}, /*index=5*/s32[2,2]{1,0:T(2,128)}, s32[]{:T(128)}, s32[]{:T(128)}) while((s32[]{:T(128)}, f32[2,12,12]{2,1,0:T(8,128)}, f32[2,12]{1,0:T(2,128)}, bf16[2,64,512]{2,1,0:T(8,128)(2,1)}, ...), condition=%wide.region_3.4_spmd, body=%wide.region_2.3_spmd.sunk | while | flops 62232948 | bytes 19173560 | solution.py:135
  70.1 3.9 concatenate.149
  76.6 2.8 fusion.159
  91.4 3.9 concatenate.149
  97.9 2.9 fusion.159
  104.2 4.9 collective-permute-start.1
  111.8 2.6 collective-permute-start.4
  115.6 42.6 %while.47 = (s32[]{:T(128)}, f32[2,12,12]{2,1,0:T(8,128)}, f32[2,12]{1,0:T(2,128)}, bf16[2,64,512]{2,1,0:T(8,128)(2,1)}, bf16[2,64,512]{2,1,0:T(8,128)(2,1)}, /*index=5*/s32[2,2]{1,0:T(2,128)}, s32[]{:T(128)}, s32[]{:T(128)}) while((s32[]{:T(128)}, f32[2,12,12]{2,1,0:T(8,128)}, f32[2,12]{1,0:T(2,128)}, bf16[2,64,512]{2,1,0:T(8,128)(2,1)}, ...), condition=%wide.region_5.6_spmd, body=%wide.region_4.5_spmd.sunk | while | flops 62232948 | bytes 19173560 | solution.py:135
  126.4 3.9 concatenate.150
  132.9 2.8 fusion.167
  147.6 3.9 concatenate.150
  154.1 2.9 fusion.167
  159.8 3.8 collective-permute-start.3
  165.6 3.6 collective-permute-start.5
  173.6 4.2 collective-permute-start.6
  178.5 4.4 collective-permute-start.9
  184.5 2.7 collective-permute-done.8
  189.6 81.5 %all-reduce.15 = (f32[]{:T(128)}, f32[]{:T(128)}) all-reduce(f32[]{:T(128)} %get-tuple-element.319, f32[]{:T(128)} %get-tuple-element.318), channel_id=1, replica_groups=mesh['sec'=8,'tile'=32] {'sec','tile'}, use_global_device_ids=true, to_apply=%region_7.8 | all-reduce | flops 2 | bytes 16 | tf_op jit(solution)/shard_map/psum | solution.py:142
  273.4 72.6 %psum.44 = f32[]{:T(128)} all-reduce(f32[]{:T(128)} %multiply_reduce_fusion.3), channel_id=1, replica_groups=mesh['sec'=8,'tile'=32] {'sec','tile'}, use_global_device_ids=true, to_apply=%region_11.12 | all-reduce | flops 1 | bytes 8 | tf_op jit(solution)/shard_map/psum | solution.py:142
  350.4 3.0 collective-permute-start.12
  358.3 2.7 collective-permute-done.14
  363.3 79.7 %psum.45 = f32[]{:T(128)} all-reduce(f32[]{:T(128)} %get-tuple-element.372), channel_id=1, replica_groups=mesh['sec'=8,'tile'=32] {'sec','tile'}, use_global_device_ids=true, to_apply=%region_13.14 | all-reduce | flops 1 | bytes 8 | tf_op jit(solution)/shard_map/psum | solution.py:197
  445.2 73.3 %psum.46 = f32[]{:T(128)} all-reduce(f32[]{:T(128)} %multiply_reduce_fusion.1), channel_id=1, replica_groups=mesh['sec'=8,'tile'=32] {'sec','tile'}, use_global_device_ids=true, to_apply=%region_15.16 | all-reduce | flops 1 | bytes 8 | tf_op jit(solution)/shard_map/psum | solution.py:142
  523.0 3.0 collective-permute-start.16
  530.9 2.7 collective-permute-done.18
  536.0 79.7 %psum.47 = f32[]{:T(128)} all-reduce(f32[]{:T(128)} %get-tuple-element.360), channel_id=1, replica_groups=mesh['sec'=8,'tile'=32] {'sec','tile'}, use_global_device_ids=true, to_apply=%region_17.18 | all-reduce | flops 1 | bytes 8 | tf_op jit(solution)/shard_map/psum | solution.py:197
  (350 shorter events, 139.6 us)
Async XLA Ops:
  0.6 8.4 %copy-start.8 = (s32[1,1,2,3]{3,2,1,0:T(2,128)S(1)}, s32[1,1,2,3]{3,2,1,0:T(2,128)}, u32[]{:S(2)}) copy-start(s32[1,1,2,3]{3,2,1,0:T(2,128)} %param.11) | copy-start | bytes 76
  0.6 9.1 %copy-start.6 = (s32[1,1,2,3,2]{3,4,2,1,0:T(2,128)S(1)}, s32[1,1,2,3,2]{3,4,2,1,0:T(2,128)}, u32[]{:S(2)}) copy-start(s32[1,1,2,3,2]{3,4,2,1,0:T(2,128)} %param.12) | copy-start | bytes 148
  2.6 55.5 %collective-permute-start = (bf16[2,64,512]{2,1,0:T(8,128)(2,1)}, bf16[2,64,512]{2,1,0:T(8,128)(2,1)}, u32[]{:S(2)}, u32[]{:S(2)}) collective-permute-start(bf16[2,64,512]{2,1,0:T(8,128)(2,1)} %get-tuple-element.494), channel_id=1, source_target_pairs={{1,0},{2,1},{3,2},{4,3},{5,4},{6,5},{7,6},{8,7},{9,8},{10,9},{11,1... | collective-permute-start | bytes 393224 | tf_op jit(solution)/shard_map/ppermute | solution.py:15
  3.9 110.5 %collective-permute-start.2 = (bf16[2,64,512]{2,1,0:T(8,128)(2,1)}, bf16[2,64,512]{2,1,0:T(8,128)(2,1)}, u32[]{:S(2)}, u32[]{:S(2)}) collective-permute-start(bf16[2,64,512]{2,1,0:T(8,128)(2,1)} %get-tuple-element.732), channel_id=1, source_target_pairs={{32,0},{64,32},{96,64},{128,96},{160,128},{192,160},{224,192},{33,... | collective-permute-start | bytes 393224 | tf_op jit(solution)/shard_map/ppermute | solution.py:15
  29.0 2.8 copy-start.10
  49.6 3.0 copy-start.10
  53.9 5.4 copy-start.9
  76.6 2.8 copy-start.12
  95.3 2.6 copy-start.2
  97.9 3.0 copy-start.12
  102.8 7.1 %copy-start.7 = (f32[12,2]{0,1:T(2,128)}, f32[12,2]{0,1:T(2,128)S(1)}, u32[]{:S(2)}) copy-start(f32[12,2]{0,1:T(2,128)S(1)} %multiply_bitcast_fusion.40) | copy-start | bytes 292
  103.6 5.6 copy-start
  104.2 61.4 %collective-permute-start.1 = (f32[6,2]{0,1:T(2,128)}, f32[6,2]{0,1:T(2,128)}, u32[]{:S(2)}, u32[]{:S(2)}) collective-permute-start(f32[6,2]{0,1:T(2,128)} %slice.471), channel_id=1, source_target_pairs={{0,1},{1,2},{2,3},{3,4},{4,5},{5,6},{6,7},{7,8},{8,9},{9,10},{10,1... | collective-permute-start | bytes 152 | tf_op jit(solution)/shard_map/ppermute | solution.py:15
  109.8 78.3 %collective-permute-start.10 = (f32[6,6,2]{1,0,2:T(8,128)}, f32[6,6,2]{1,0,2:T(8,128)}, u32[]{:S(2)}, u32[]{:S(2)}) collective-permute-start(f32[6,6,2]{1,0,2:T(8,128)} %get-tuple-element.496), channel_id=1, source_target_pairs={{0,1},{1,2},{2,3},{3,4},{4,5},{5,6},{6,7},{7,8},{8,9},{9,10},{10,1... | collective-permute-start | bytes 872 | tf_op jit(solution)/shard_map/ppermute | solution.py:15
  111.8 58.1 %collective-permute-start.4 = (f32[6,6,2]{1,0,2:T(8,128)}, f32[6,6,2]{1,0,2:T(8,128)}, u32[]{:S(2)}, u32[]{:S(2)}) collective-permute-start(f32[6,6,2]{1,0,2:T(8,128)} %get-tuple-element.497), channel_id=1, source_target_pairs={{0,1},{1,2},{2,3},{3,4},{4,5},{5,6},{6,7},{7,8},{8,9},{9,10},{10,1... | collective-permute-start | bytes 872 | tf_op jit(solution)/shard_map/ppermute | solution.py:15
  132.8 2.8 copy-start.14
  154.0 3.0 copy-start.14
  159.8 9.4 %collective-permute-start.3 = (f32[6,2]{0,1:T(2,128)S(1)}, f32[6,2]{0,1:T(2,128)S(1)}, u32[]{:S(2)}, u32[]{:S(2)}) collective-permute-start(f32[6,2]{0,1:T(2,128)S(1)} %slice.476), channel_id=1, source_target_pairs={{0,32},{32,64},{64,96},{96,128},{128,160},{160,192},{192,224},{1,3... | collective-permute-start | bytes 152 | tf_op jit(solution)/shard_map/ppermute | solution.py:15
  163.7 20.7 %collective-permute-start.11 = (f32[6,6,2]{1,0,2:T(8,128)S(1)}, f32[6,6,2]{1,0,2:T(8,128)S(1)}, u32[]{:S(2)}, u32[]{:S(2)}) collective-permute-start(f32[6,6,2]{1,0,2:T(8,128)S(1)} %get-tuple-element.498), channel_id=1, source_target_pairs={{0,32},{32,64},{64,96},{96,128},{128,160},{160,192},{192,224},{1,3... | collective-permute-start | bytes 872 | tf_op jit(solution)/shard_map/ppermute | solution.py:15
  165.6 4.4 collective-permute-start.5
  171.7 6.4 %collective-permute-start.7 = (f32[6,1,1,2]{0,3,2,1:T(2,128)S(1)}, f32[6,1,1,2]{0,3,2,1:T(2,128)S(1)}, u32[]{:S(2)}, u32[]{:S(2)}) collective-permute-start(f32[6,1,1,2]{0,3,2,1:T(2,128)S(1)} %bitcast.738), channel_id=1, source_target_pairs={{32,0},{64,32},{96,64},{128,96},{160,128},{192,160},{224,192},{33,... | collective-permute-start | bytes 152 | tf_op jit(solution)/shard_map/ppermute | solution.py:28
  173.6 4.9 collective-permute-start.6
  178.5 9.6 %collective-permute-start.9 = (f32[6,3,1,2]{0,3,2,1:T(2,128)S(1)}, f32[6,3,1,2]{0,3,2,1:T(2,128)S(1)}, u32[]{:S(2)}, u32[]{:S(2)}) collective-permute-start(f32[6,3,1,2]{0,3,2,1:T(2,128)S(1)} %pad_maximum_fusion), channel_id=1, source_target_pairs={{0,1},{1,2},{2,3},{3,4},{4,5},{5,6},{6,7},{7,8},{8,9},{9,10},{10,1... | collective-permute-start | bytes 440 | tf_op jit(solution)/shard_map/ppermute | solution.py:26
  182.9 4.3 collective-permute-start.8
  347.8 5.8 collective-permute-start.13
  350.4 3.7 collective-permute-start.12
  354.1 7.8 %collective-permute-start.15 = (f32[6,3,1,2]{0,3,2,1:T(2,128)S(1)}, f32[6,3,1,2]{0,3,2,1:T(2,128)S(1)}, u32[]{:S(2)}, u32[]{:S(2)}) collective-permute-start(f32[6,3,1,2]{0,3,2,1:T(2,128)S(1)} %pad_maximum_fusion.1), channel_id=1, source_target_pairs={{0,1},{1,2},{2,3},{3,4},{4,5},{5,6},{6,7},{7,8},{8,9},{9,10},{10,1... | collective-permute-start | bytes 440 | tf_op jit(solution)/shard_map/ppermute | solution.py:26
  356.6 4.3 collective-permute-start.14
  520.4 5.8 collective-permute-start.17
  523.0 3.7 collective-permute-start.16
  526.7 7.8 %collective-permute-start.19 = (f32[6,3,1,2]{0,3,2,1:T(2,128)S(1)}, f32[6,3,1,2]{0,3,2,1:T(2,128)S(1)}, u32[]{:S(2)}, u32[]{:S(2)}) collective-permute-start(f32[6,3,1,2]{0,3,2,1:T(2,128)S(1)} %pad_maximum_fusion.2), channel_id=1, source_target_pairs={{0,1},{1,2},{2,3},{3,4},{4,5},{5,6},{6,7},{7,8},{8,9},{9,10},{10,1... | collective-permute-start | bytes 440 | tf_op jit(solution)/shard_map/ppermute | solution.py:26
  529.2 4.3 collective-permute-start.18
  (14 other events, 14.4 us)
where the time goes:
time: 622 us; the launch traced here: 618 us
  blocking collectives  387 us (62%)
  local copies, waits for them, and re-layouts  81.8 us (13%)
  starting transfers between devices  55.8 us (9%)
  matrix products  40.5 us (7%)
  other arithmetic  35 us (6%)
  waiting for transfers between devices  9.58 us (2%)
  between operations  7.72 us (1%)
    psum x3, blocking collectives, squares_sum(): return lax.psum(jnp.sum(residual * scaled), ('sec', 'tile'))  227 us
    psum x2, blocking collectives, shards(): step_size = rho_now / lax.psum(jnp.sum(direction * result), ('sec', 'tile'))  159 us
    while x118, local copies, waits for them, and re-layouts  31.9 us
    ppermute x8, starting transfers between devices, passed_along(): return lax.ppermute(shard, axis, pairs)  25.2 us
    concatenate x6, local copies, waits for them, and re-layouts, pair_block(): jnp.concatenate([jacobian_rows(first, zero, zero), -jacobian_rows(second,...  23.2 us
    ppermute x6, starting transfers between devices, with_halo(): lax.ppermute(tail, axis, [(i, (i + 1) % count) for i in range(ends)])  19.6 us
    dot_general x6, matrix products, pair_block(): jnp.dot(jacobian, jacobian.T, precision=highest, preferred_element_type=j...  17.2 us
    dot_general x6, matrix products, pair_block(): jnp.dot(jacobian, misfit, precision=highest, preferred_element_type=jnp.f...  15.5 us
  transfers between devices with their start and end apart: 20, of which 6 were waited for; matrix products, arithmetic and copies ran while one was open for 23% of the time, Pallas kernels for 0%

commit v1 on v0

v1 whole, which is shorter than its diff:
```python
import functools

import jax
import jax.numpy as jnp
from jax import lax
from jax.experimental import pallas as pl
from jax.experimental.pallas import tpu as pltpu
from jax.sharding import Mesh, PartitionSpec as P

ITERS = 3
H, W = 64, 512
F32 = jnp.float32
LANES = 128
SELF_H, SELF_T, SELF_B, SELF_P = 0, 3, 6, 9
CROSS = {"down": 12, "sec": 16}
CROSS_RIGHT = 20
PULL_RIGHT = 22
PULL = {"down": 24, "sec": 28}
META_LANE = 44
SCALE = 2.0**-17

VMEM = pl.BlockSpec(memory_space=pltpu.VMEM)
SMEM = pl.BlockSpec(memory_space=pltpu.SMEM)


def iota(shape, axis):
    return lax.broadcasted_iota(jnp.int32, shape, axis)


def store_gradients(image, gx_ref, gy_ref):
    col = iota((H, W), 1)
    row = iota((H, W), 0)
    ahead = jnp.where(col < W - 1, pltpu.roll(image, W - 1, 1), 0.0)
    behind = jnp.where(col > 0, pltpu.roll(image, 1, 1), 0.0)
    gx_ref[...] = ahead - behind
    below = jnp.where(row < H - 1, pltpu.roll(image, H - 1, 0), 0.0)
    above = jnp.where(row > 0, pltpu.roll(image, 1, 0), 0.0)
    gy_ref[...] = below - above


def row_moments(sums, level):
    s = iota((8, LANES), 0).astype(F32)
    c = 0.5 + s / H
    out = [sums[0], c * sums[0] - sums[1] * 0.125]
    if level == 3:
        out.append(c * c * sums[0] - (0.25 * c) * sums[1] + (2.0 * sums[2] - sums[1]) * (1.0 / 64.0))
    return out


def accumulate(fields, level):
    sums = None
    for k in range(8):
        values = fields(k)
        if sums is None:
            sums = [[v] * lv for v, lv in zip(values, level)]
            continue
        new = []
        for v, old, lv in zip(values, sums, level):
            now = [old[0] + v]
            for q in range(1, lv):
                now.append(old[q] + now[q - 1])
            new.append(now)
        sums = new
    return [row_moments(s, lv) for s, lv in zip(sums, level)]


def tree8(vs):
    s = iota((8, LANES), 0)
    m4 = s < 4
    w = []
    for i in range(4):
        x = jnp.where(m4, vs[i], vs[i + 4])
        y = jnp.where(m4, vs[i + 4], vs[i])
        w.append(x + pltpu.roll(y, 4, 0))
    m2 = (s & 2) == 0
    z = []
    for i in range(2):
        x = jnp.where(m2, w[i], w[i + 2])
        y = jnp.where(m2, w[i + 2], w[i])
        z.append(x + jnp.where(m2, pltpu.roll(y, 6, 0), pltpu.roll(y, 2, 0)))
    m1 = (s & 1) == 0
    x = jnp.where(m1, z[0], z[1])
    y = jnp.where(m1, z[1], z[0])
    return x + jnp.where(m1, pltpu.roll(y, 7, 0), pltpu.roll(y, 1, 0))


def put_group(group, lt, found, low_ref, high_ref):
    lanes = pl.ds(lt * LANES, LANES)
    order = [found[(f, t)] for f in range(4) for t in range(2)]
    for q in range(3):
        if not any(len(v) > q for v in order):
            continue
        vs = [v[q] if len(v) > q else jnp.zeros((8, LANES), F32) for v in order]
        total = tree8(vs)
        if q < 2:
            low_ref[pl.ds(64 * q + 8 * group, 8), lanes] = total
        else:
            high_ref[pl.ds(64 + 8 * group, 8), lanes] = total


def column_moments(low_ref, high_ref):
    r = iota((8, W), 0)
    u = iota((8, W), 1).astype(F32) / W - 0.5
    w = jnp.where(r == 0, 1.0, jnp.where(r == 1, u, u * u)) * SCALE
    dims = (((1,), (1,)), ((), ()))
    low = lax.dot_general(w, low_ref[...], dims, precision=lax.Precision.HIGHEST, preferred_element_type=F32)
    ones = jnp.full((8, W), SCALE, F32)
    high = lax.dot_general(ones, high_ref[...], dims, precision=lax.Precision.HIGHEST, preferred_element_type=F32)
    row = iota((8, LANES), 0)
    lane = iota((8, LANES), 1)
    return jnp.where((row == 2) & (lane >= 64), high, jnp.where(row < 3, low, 0.0))


def pair_fields(gxa, gya, gxb, gyb, misfit, lanes):
    def fields(k):
        rows = pl.ds(8 * k, 8)
        xa, ya, xb, yb, m = (ref[rows, lanes] for ref in (gxa, gya, gxb, gyb, misfit))
        return [xa * xb, xa * yb, ya * xb, ya * yb, xa * m, ya * m, xb * m, yb * m]

    return fields


def self_fields(gx, gy, lanes):
    def fields(k):
        rows = pl.ds(8 * k, 8)
        x, y = gx[rows, lanes], gy[rows, lanes]
        return [x * x, x * y, y * y]

    return fields


PAIR_LEVEL = (3, 3, 3, 3, 2, 2, 2, 2)


def cut_kernel(strips, tops, patches, sems):
    copies = []
    for t in range(2):
        copies.append(pltpu.make_async_copy(strips.at[0, 0, t, 2], tops.at[t], sems.at[t]))
        copies.append(pltpu.make_async_copy(strips.at[0, 0, t, 4], patches.at[t], sems.at[2 + t]))
    for copy in copies:
        copy.start()
    for copy in copies:
        copy.wait()


def own_kernel(strips, mask, offset, stiff, out, grad, misfit, low, high):
    low[...] = jnp.zeros_like(low)
    high[...] = jnp.zeros_like(high)
    kinds = ((1, 0), (2, 2), (3, 3), (4, 4))
    for kind, images in enumerate(kinds):
        for t in range(2):
            image = strips[0, 0, t, images[t]].astype(F32)
            store_gradients(image, grad.at[kind, t, 0], grad.at[kind, t, 1])
    misfit[...] = strips[0, 0, 0, 1].astype(F32) - strips[0, 0, 1, 0].astype(F32)
    for lt in range(4):
        lanes = pl.ds(lt * LANES, LANES)
        found = {}
        for kind in range(4):
            for t in range(2):
                got = accumulate(self_fields(grad.at[kind, t, 0], grad.at[kind, t, 1], lanes), (3, 3, 3))
                for n in range(3):
                    found[(3 * kind + n, t)] = got[n]
        for group in range(3):
            put_group(group, lt, {(f, t): found[(4 * group + f, t)] for f in range(4) for t in range(2)}, low, high)
        got = accumulate(
            pair_fields(grad.at[0, 0, 0], grad.at[0, 0, 1], grad.at[0, 1, 0], grad.at[0, 1, 1], misfit, lanes),
            PAIR_LEVEL,
        )
        right = {(0, 0): got[0], (0, 1): got[1], (1, 0): got[2], (1, 1): got[3],
                 (2, 0): got[4], (3, 0): got[5], (2, 1): got[6], (3, 1): got[7]}
        put_group(5, lt, right, low, high)
    total = column_moments(low, high)
    row = iota((8, LANES), 0)
    lane = iota((8, LANES), 1)
    meta = jnp.zeros((8, LANES), F32)
    for t in range(2):
        scalars = [mask[0, 0, t, k].astype(F32) for k in range(3)]
        scalars += [offset[0, 0, t, d, k].astype(F32) for k in range(3) for d in range(2)]
        scalars.append(stiff[0, 0, t])
        for n, value in enumerate(scalars):
            meta = jnp.where(lane == META_LANE + 2 * n + t, value, meta)
    out[...] = jnp.where((row == 2) & (lane >= META_LANE) & (lane < 64), meta, total)


def pairs_kernel(strips, lower, later, own, out, grad, misfit, low, high):
    low[...] = jnp.zeros_like(low)
    high[...] = jnp.zeros_like(high)
    for kind, image_a, second in ((0, 3, lower), (1, 4, later)):
        for t in range(2):
            a = strips[0, 0, t, image_a].astype(F32)
            b = second[t].astype(F32)
            store_gradients(a, grad.at[kind, t, 0], grad.at[kind, t, 1])
            store_gradients(b, grad.at[kind, t, 2], grad.at[kind, t, 3])
            misfit[kind, t] = a - b
        for lt in range(4):
            lanes = pl.ds(lt * LANES, LANES)
            cross, pull = {}, {}
            for t in range(2):
                g = [grad.at[kind, t, n] for n in range(4)]
                got = accumulate(pair_fields(*g, misfit.at[kind, t], lanes), PAIR_LEVEL)
                for n in range(4):
                    cross[(n, t)] = got[n]
                    pull[(n, t)] = got[4 + n]
            put_group(3 + kind, lt, cross, low, high)
            put_group(6 + kind, lt, pull, low, high)
    total = column_moments(low, high)
    row = iota((8, LANES), 0)
    lane = iota((8, LANES), 1)
    is_meta = (row == 2) & (lane >= META_LANE) & (lane < 64)
    out[...] = own[...] + jnp.where(is_meta, 0.0, total)


def solve_kernel(mine, theirs, update_out, residual_out, table):
    core = lax.axis_index("core")
    place = lax.axis_index("y") * 32 + lax.axis_index("tile")
    sub = iota((8, LANES), 0)
    lane = iota((8, LANES), 1)
    c0 = (sub & 1) == 0
    t0 = (sub & 2) == 0
    live = sub < 4
    row = lane & 31
    sec = 2 * (lane >> 5) + (sub & 1)
    for r in range(3):
        a = mine[pl.ds(r, LANES, stride=4), :]
        b = theirs[pl.ds(r, LANES, stride=4), :]
        first = jnp.where(core == 0, a, b)
        second = jnp.where(core == 0, b, a)
        table[pl.ds(256 * r, LANES, stride=2), :] = first.T
        table[pl.ds(256 * r + 1, LANES, stride=2), :] = second.T

    def read(r, h, f):
        return table[pl.ds(256 * r + 128 * h + 4 * f, 8), :]

    def low3(f):
        return read(1, 0, f), read(0, 1, f), read(0, 0, f)

    def all6(f):
        return (read(2, 0, f), read(1, 1, f), read(1, 0, f), read(2, 1, f), read(0, 1, f), read(0, 0, f))

    def meta(n):
        return read(2, 0, META_LANE // 2 + n)

    def swap_tile(x):
        return jnp.where(t0, pltpu.roll(x, 6, 0), pltpu.roll(x, 2, 0))

    def swap_core(x):
        return jnp.where(c0, pltpu.roll(x, 7, 0), pltpu.roll(x, 1, 0))

    def row_from_next(x):
        return pltpu.roll(x, LANES - 1, 1)

    def row_to_next(x):
        return pltpu.roll(x, 1, 1)

    def sec_from_next(x):
        x = swap_core(x)
        return jnp.where(c0, x, pltpu.roll(x, LANES - 32, 1))

    def sec_to_next(x):
        x = swap_core(x)
        return jnp.where(c0, pltpu.roll(x, 32, 1), x)

    zero = jnp.zeros((8, LANES), F32)
    exists_right = jnp.where((meta(0) == 1.0) & t0, 1.0, 0.0)
    exists_right = jnp.where(t0, exists_right, swap_tile(exists_right))
    exists_down = jnp.where((meta(1) == 1.0) & (row < 31), 1.0, 0.0)
    exists_sec = jnp.where((meta(2) == 1.0) & (sec < 7), 1.0, 0.0)
    du = [meta(3 + 2 * k) * (1.0 / W) for k in range(3)]
    dv = [meta(4 + 2 * k) * (1.0 / H) for k in range(3)]
    stiffness = meta(9)
    au = jnp.where(t0, zero, swap_tile(du[0]))
    av = jnp.where(t0, zero, swap_tile(dv[0]))
    bu = jnp.where(t0, du[0], zero)
    bv = jnp.where(t0, dv[0], zero)

    def shifted(m, a, b):
        uu, uv, u, vv, v, one = m
        return (uu + 2.0 * a * u + a * a * one, uv + a * v + b * u + a * b * one, u + a * one,
                vv + 2.0 * b * v + b * b * one, v + b * one, one)

    down_up, down_du, down_dv = row_to_next(exists_down), row_to_next(du[1]), row_to_next(dv[1])
    sec_up, sec_du, sec_dv = sec_to_next(exists_sec), sec_to_next(du[2]), sec_to_next(dv[2])
    blocks = []
    for n in range(3):
        total = [exists_right * m for m in shifted(all6(SELF_H + n), au, av)]
        for f, ex, off in ((SELF_T, down_up, (down_du, down_dv)), (SELF_B, exists_down, None),
                           (SELF_P, exists_sec, None), (SELF_P, sec_up, (sec_du, sec_dv))):
            m = all6(f + n)
            if off is not None:
                m = shifted(m, *off)
            total = [x + ex * y for x, y in zip(total, m)]
        if n != 1:
            total = [x + stiffness if i in (0, 3, 5) else x for i, x in enumerate(total)]
        blocks.append(total)
    square = ((0, 1, 2), (1, 3, 4), (2, 4, 5))
    diagonal = [[blocks[(i // 3) + (j // 3)][square[i % 3][j % 3]] for j in range(6)] for i in range(6)]

    lower = [[None] * 6 for _ in range(6)]
    scaled_col = [[None] * 6 for _ in range(6)]
    inverse_pivot = []
    work = {(i, j): diagonal[i][j] for i in range(6) for j in range(i + 1)}
    for j in range(6):
        inv = 1.0 / work[(j, j)]
        inverse_pivot.append(inv)
        for i in range(j + 1, 6):
            lower[i][j] = work[(i, j)] * inv
        for i in range(j + 1, 6):
            for k in range(j + 1, i + 1):
                work[(i, k)] = work[(i, k)] - lower[i][j] * work[(k, j)]
    inverse = [[None] * 6 for _ in range(6)]
    for j in range(6):
        for i in range(j + 1, 6):
            value = lower[i][j]
            for k in range(j + 1, i):
                value = value + lower[i][k] * inverse[k][j]
            inverse[i][j] = -value

    def precondition(v):
        mid = []
        for i in range(6):
            value = v[i]
            for j in range(i):
                value = value + inverse[i][j] * v[j]
            mid.append(value * inverse_pivot[i])
        out = []
        for i in range(6):
            value = mid[i]
            for j in range(i + 1, 6):
                value = value + inverse[j][i] * mid[j]
            out.append(value)
        return out

    def coupling(m, ex, ra, rb, ca, cb):
        uu, uv, u, vv, v, one = m
        if ra is None:
            block = [[uu + ca * u, uv + cb * u, u], [uv + ca * v, vv + cb * v, v], [u + ca * one, v + cb * one, one]]
        else:
            block = [[uu + (ra + ca) * u, uv + ra * v + cb * u, u + ra * one],
                     [uv + ca * v + rb * u, vv + (rb + cb) * v, v + rb * one],
                     [u + ca * one, v + cb * one, one]]
        return [[-(ex * x) for x in line] for line in block]

    def join(xx, xy, yx, yy):
        return [a + b for a, b in zip(xx, xy)] + [a + b for a, b in zip(yx, yy)]

    couplings = {}
    for kind, n, ex in (("down", 1, exists_down), ("sec", 2, exists_sec)):
        f = CROSS[kind]
        couplings[kind] = join(*(coupling(all6(f + i), ex, None, None, du[n], dv[n]) for i in range(4)))
    a6, b6 = all6(CROSS_RIGHT), all6(CROSS_RIGHT + 1)
    sa6, sb6 = [swap_tile(x) for x in a6], [swap_tile(x) for x in b6]

    def pick(x, y):
        return [jnp.where(t0, p, q) for p, q in zip(x, y)]

    right = (pick(a6, sa6), pick(sa6, sb6), pick(b6, a6), pick(sb6, b6))
    right = join(*(coupling(m, exists_right, au, av, bu, bv) for m in right))

    sign = jnp.where(t0, -2.0, 2.0) * exists_right
    load = []
    for n in range(2):
        u, v, one = low3(PULL_RIGHT + n)
        load += [sign * (u + au * one), sign * (v + av * one), sign * one]
    for kind, n, ex, push in (("down", 1, exists_down, row_to_next), ("sec", 2, exists_sec, sec_to_next)):
        f = PULL[kind]
        twice = 2.0 * ex
        for i in range(2):
            for j, x in enumerate(low3(f + i)):
                load[3 * i + j] = load[3 * i + j] - twice * x
            u, v, one = low3(f + 2 + i)
            for j, x in enumerate((u + du[n] * one, v + dv[n] * one, one)):
                load[3 * i + j] = load[3 * i + j] + push(twice * x)

    def times(block, vector, transpose):
        out = []
        for i in range(6):
            value = None
            for j in range(6):
                term = (block[j][i] if transpose else block[i][j]) * vector[j]
                value = term if value is None else value + term
            out.append(value)
        return out

    def multiply(vector):
        parts = [times(diagonal, vector, False)]
        parts.append(times(right, [swap_tile(x) for x in vector], False))
        parts.append(times(couplings["down"], [row_from_next(x) for x in vector], False))
        parts.append([row_to_next(x) for x in times(couplings["down"], vector, True)])
        parts.append(times(couplings["sec"], [sec_from_next(x) for x in vector], False))
        parts.append([sec_to_next(x) for x in times(couplings["sec"], vector, True)])
        return [functools.reduce(jnp.add, line) for line in zip(*parts)]

    def inner(x, y):
        total = functools.reduce(jnp.add, [a * b for a, b in zip(x, y)])
        total = jnp.where(live, total, 0.0)
        return jnp.sum(total, axis=(0, 1), keepdims=True)

    residual = load
    direction = precondition(residual)
    rho = inner(residual, direction)
    update = None
    for step in range(ITERS):
        product = multiply(direction)
        size = rho / inner(direction, product)
        if update is None:
            update = [size * d for d in direction]
        else:
            update = [x + size * d for x, d in zip(update, direction)]
        residual = [r - size * p for r, p in zip(residual, product)]
        if step < ITERS - 1:
            scaled = precondition(residual)
            rho_next = inner(residual, scaled)
            ratio = rho_next / rho
            direction = [z + ratio * d for z, d in zip(scaled, direction)]
            rho = rho_next

    here = (lane == place) & live & ((sub & 1) == core)
    for vector, out in ((update, update_out), (residual, residual_out)):
        found = zero
        for i in range(6):
            value = jnp.sum(jnp.where(here, vector[i], 0.0), axis=1, keepdims=True)
            found = jnp.where(lane == i, value, found)
        found = found + pltpu.roll(found, 7, 0)
        out[0, 0, 0:1] = found[0:1, :6]
        out[0, 0, 1:2] = found[2:3, :6]


def shards(tile_strips, pair_mask, strip_offset, stiffness):
    tiles = lax.axis_size("tile")
    chips = lax.axis_size("y") * tiles
    sections = lax.axis_size("y") * 2
    image = jax.ShapeDtypeStruct((2, H, W), tile_strips.dtype)
    tops, patches = pl.pallas_call(
        cut_kernel,
        out_shape=(image, image),
        in_specs=[pl.BlockSpec(memory_space=pltpu.HBM)],
        out_specs=(VMEM, VMEM),
        scratch_shapes=[pltpu.SemaphoreType.DMA((4,))],
        compiler_params=pltpu.CompilerParams(vmem_limit_bytes=2 << 20),
        name="cut",
    )(tile_strips)
    lower = lax.ppermute(tops, "tile", [(i + 1, i) for i in range(tiles - 1)])
    later = lax.ppermute(patches, ("y", "core"), [(i + 1, i) for i in range(sections - 1)])
    small = jax.ShapeDtypeStruct((8, LANES), F32)
    own = pl.pallas_call(
        own_kernel,
        out_shape=small,
        in_specs=[VMEM, SMEM, SMEM, SMEM],
        out_specs=VMEM,
        scratch_shapes=[pltpu.VMEM((4, 2, 2, H, W), F32), pltpu.VMEM((H, W), F32),
                        pltpu.VMEM((128, W), F32), pltpu.VMEM((128, W), F32)],
        cost_estimate=pl.CostEstimate(flops=20_000_000, bytes_accessed=700_000, transcendentals=0),
        compiler_params=pltpu.CompilerParams(vmem_limit_bytes=6 << 20),
        name="own_moments",
    )(tile_strips, pair_mask, jnp.swapaxes(strip_offset, 3, 4), stiffness)
    moments = pl.pallas_call(
        pairs_kernel,
        out_shape=small,
        in_specs=[VMEM] * 4,
        out_specs=VMEM,
        scratch_shapes=[pltpu.VMEM((2, 2, 4, H, W), F32), pltpu.VMEM((2, 2, H, W), F32),
                        pltpu.VMEM((128, W), F32), pltpu.VMEM((128, W), F32)],
        cost_estimate=pl.CostEstimate(flops=20_000_000, bytes_accessed=900_000, transcendentals=0),
        compiler_params=pltpu.CompilerParams(vmem_limit_bytes=6 << 20),
        name="pair_moments",
    )(tile_strips, lower, later, own)
    sent = jnp.broadcast_to(moments[None, :4], (chips, 4, LANES))
    mine = lax.all_to_all(sent, ("y", "tile"), 0, 0)
    theirs = lax.ppermute(mine, "core", [(0, 1), (1, 0)])
    out = jax.ShapeDtypeStruct((1, 1, 2, 6), F32)
    outs = pl.pallas_call(
        solve_kernel,
        out_shape=(out, out),
        in_specs=[VMEM] * 2,
        out_specs=(VMEM, VMEM),
        scratch_shapes=[pltpu.VMEM((3 * 256 + 8, LANES), F32)],
        compiler_params=pltpu.CompilerParams(vmem_limit_bytes=4 << 20),
        name="solve",
    )(mine.reshape(chips * 4, LANES), theirs.reshape(chips * 4, LANES))
    return tuple(jnp.transpose(x, (3, 0, 1, 2)) for x in outs)


def solution(mesh):
    fine = Mesh(mesh.devices.reshape(4, 2, 32), ("y", "core", "tile"))
    sec = ("y", "core")
    return jax.shard_map(
        shards,
        mesh=fine,
        in_specs=(
            P(sec, "tile", None, None, None, None),
            P(sec, "tile", None, None),
            P(sec, "tile", None, None, None),
            P(sec, "tile", None),
        ),
        out_specs=(P(None, sec, "tile", None), P(None, sec, "tile", None)),
        check_vma=False,
    )
```

time: 622 us -> 47.7 us (0.08)
  blocking collectives: 387 us -> 28.7 us
  local copies, waits for them, and re-layouts: 81.8 us -> 1.17 us
  starting transfers between devices: 55.8 us -> 9.38 us
  matrix products: 40.5 us -> 0 us
  other arithmetic: 35 us -> 0 us
  waiting for transfers between devices: 9.58 us -> 1.19 us
  between operations: 7.72 us -> 0.75 us
  Pallas kernels: 0 us -> 6.4 us
    psum x5 -> x0, blocking collectives: 387 us -> none  [the longest x3 227 us: squares_sum(): return lax.psum(jnp.sum(residual * scaled), ('sec', 'tile'))]
    ppermute x20 -> x3, starting transfers between devices: 55.8 us -> 9.38 us  [the longest x1 5.11 us: shards(): lax.ppermute(patches, ('y', 'core'), [(i + 1, i) for i in range(sections...]
    dot_general x33 -> x0, matrix products: 40.5 us -> none  [the longest x6 17.2 us: pair_block(): jnp.dot(jacobian, jacobian.T, precision=highest, preferred_element_type=j...]
    while x118 -> x0, local copies, waits for them, and re-layouts: 31.9 us -> none
    all_to_all x0 -> x1, blocking collectives: none -> 28.7 us  [shards(): mine = lax.all_to_all(sent, ('y', 'tile'), 0, 0)]
    concatenate x10 -> x0, local copies, waits for them, and re-layouts: 23.9 us -> none  [the longest x6 23.2 us: pair_block(): jnp.concatenate([jacobian_rows(first, zero, zero), -jacobian_rows(second,...]
    mul x30 -> x0, other arithmetic: 12.3 us -> none  [the longest x12 3.9 us: jacobian_rows(): along_x * coord_u]
    another operation x18 -> x0, local copies, waits for them, and re-layouts: 11 us -> none  [the longest x6 7.47 us: jacobian_rows(): jnp.stack([along_x * coord_u, along_x * coord_v, along_x, along_y * coord...]
  transfers between devices with their start and end apart: 20 -> 3, of which waited for: 6 -> 1; matrix products, arithmetic and copies ran while one was open for 23% -> 0% of each run, Pallas kernels for 0% -> 5%
where the time goes in v1:
time: 47.7 us; the launch traced here: 47.5 us
  blocking collectives  28.7 us (60%)
  starting transfers between devices  9.38 us (20%)
  Pallas kernels  6.4 us (13%)
  waiting for transfers between devices  1.19 us (2%)
  local copies, waits for them, and re-layouts  1.17 us (2%)
  between operations  0.75 us (2%)
    all_to_all x1, blocking collectives, shards(): mine = lax.all_to_all(sent, ('y', 'tile'), 0, 0)  28.7 us
    ppermute x1, starting transfers between devices, shards(): lax.ppermute(patches, ('y', 'core'), [(i + 1, i) for i in range(sections...  5.11 us
    ppermute x1, starting transfers between devices, shards(): theirs = lax.ppermute(mine, 'core', [(0, 1), (1, 0)])  2.98 us
    pallas_call x1, Pallas kernels, shards(): pl.pallas_call(own_kernel, out_shape=small, in_specs=[VMEM, SMEM, SMEM, S...  2.4 us
    pallas_call x1, Pallas kernels, shards(): pl.pallas_call(solve_kernel, out_shape=(out, out), in_specs=[VMEM] * 2, o...  1.96 us
    pallas_call x1, Pallas kernels, shards(): pl.pallas_call(pairs_kernel, out_shape=small, in_specs=[VMEM] * 4, out_sp...  1.69 us
    ppermute x1, starting transfers between devices, shards(): lower = lax.ppermute(tops, 'tile', [(i + 1, i) for i in range(tiles - 1)])  1.29 us
    ppermute x1, waiting for transfers between devices, shards(): theirs = lax.ppermute(mine, 'core', [(0, 1), (1, 0)])  1.16 us
  transfers between devices with their start and end apart: 3, of which 1 were waited for; matrix products, arithmetic and copies ran while one was open for 0% of the time, Pallas kernels for 5%

profile of v1, /device:TPU:1, one launch (start us, length us, event | category | flops | bytes accessed | tf_op | source)
XLA Modules:
  0.0 47.5 jit_solution(1393381531772745188)
XLA Ops:
  0.6 0.0 copy-start
  0.6 1.1 %copy-done = bf16[1,1,2,5,64,512]{5,4,3,2,1,0:T(8,128)(2,1)S(1)} copy-done((bf16[1,1,2,5,64,512]{5,4,3,2,1,0:T(8,128)(2,1)S(1)}, bf16[1,1,2,5,64,512]{5,4,3,2,1,0:T(8,128)(2,1)}, u32[]{:S(2)}) %copy-start) | copy-done | bytes 655384
  1.7 0.0 copy-start.1
  1.7 0.4 cut.1
  2.1 0.0 copy-start.2
  2.1 1.3 %collective-permute-start = (bf16[2,64,512]{2,1,0:T(8,128)(2,1)S(1)}, bf16[2,64,512]{2,1,0:T(8,128)(2,1)S(1)}, u32[]{:S(2)}, u32[]{:S(2)}) collective-permute-start(bf16[2,64,512]{2,1,0:T(8,128)(2,1)S(1)} %get-tuple-element.6), channel_id=1, source_target_pairs={{1,0},{2,1},{3,2},{4,3},{5,4},{6,5},{7,6},{8,7},{9,8},{10,9},{11,1... | collective-permute-start | bytes 393224 | tf_op jit(solution)/shard_map/ppermute | solution.py:442
  3.4 0.0 copy-start.3
  3.4 0.0 copy-start.4
  3.4 5.1 %collective-permute-start.1 = (bf16[2,64,512]{2,1,0:T(8,128)(2,1)S(1)}, bf16[2,64,512]{2,1,0:T(8,128)(2,1)S(1)}, u32[]{:S(2)}, u32[]{:S(2)}) collective-permute-start(bf16[2,64,512]{2,1,0:T(8,128)(2,1)S(1)} %get-tuple-element.7), channel_id=1, source_target_pairs={{32,0},{64,32},{96,64},{128,96},{160,128},{192,160},{224,192},{33,... | collective-permute-start | bytes 393224 | tf_op jit(solution)/shard_map/ppermute | solution.py:443
  8.5 0.0 copy-done.1
  8.5 0.0 copy-done.2
  8.6 0.0 copy-done.3
  8.6 0.0 copy-done.4
  8.6 2.4 %own_moments.1.own = f32[8,128]{1,0:T(8,128)S(1)} custom-call(bf16[1,1,2,5,64,512]{5,4,3,2,1,0:T(8,128)(2,1)S(1)} %copy-done.1, s32[1,1,2,3]{3,2,1,0:T(2,128)S(1)} %copy-done.3, s32[1,1,2,2,3]{4,3,2,1,0:T(2,128)S(1)} %bitcast.7, f32[1,1,2]{2,1,0:T(1,128)S(1)} %copy-done.4), custom_call_target="tpu_custom_call" | custom-call | flops 20000000 | bytes 700000 | tf_op jit(solution)/shard_map/own_moments/pallas_call | solution.py:445
  11.0 0.0 collective-permute-done.lower
  11.0 0.0 collective-permute-done.1.later
  11.0 1.7 %pair_moments.1 = f32[8,128]{1,0:T(8,128)S(1)} custom-call(bf16[1,1,2,5,64,512]{5,4,3,2,1,0:T(8,128)(2,1)S(1)} %copy-done.1, bf16[2,64,512]{2,1,0:T(8,128)(2,1)S(1)} %collective-permute-done.lower, bf16[2,64,512]{2,1,0:T(8,128)(2,1)S(1)} %collective-permute-done.1.later, f32[8,128]{1,0:T(8,128)S(1)} %own_moments.1.own), custom_call_target="tpu_custom_call" | custom-call | flops 20000000 | bytes 900000 | tf_op jit(solution)/shard_map/pair_moments/pallas_call | solution.py:456
  12.7 0.1 broadcast_in_dim.2
  12.8 28.7 %all_to_all.5 = f32[128,4,128]{2,1,0:T(4,128)S(1)} all-to-all(f32[128,4,128]{2,1,0:T(4,128)S(1)} %broadcast_in_dim.2), channel_id=1, replica_groups=mesh['y'=4,'core'=2,'tile'=32] {'y','tile'}, dimensions={0} | all-to-all | bytes 524288 | tf_op jit(solution)/shard_map/all_to_all | solution.py:468
  41.4 3.0 %collective-permute-start.2 = (f32[128,4,128]{2,1,0:T(4,128)S(1)}, f32[128,4,128]{2,1,0:T(4,128)S(1)}, u32[]{:S(2)}, u32[]{:S(2)}) collective-permute-start(f32[128,4,128]{2,1,0:T(4,128)S(1)} %all_to_all.5), channel_id=1, source_target_pairs={{0,32},{32,0},{1,33},{33,1},{2,34},{34,2},{3,35},{35,3},{4,36},{36... | collective-permute-start | bytes 786440 | tf_op jit(solution)/shard_map/ppermute | solution.py:469
  44.4 1.2 %collective-permute-done.2 = f32[128,4,128]{2,1,0:T(4,128)S(1)} collective-permute-done((f32[128,4,128]{2,1,0:T(4,128)S(1)}, f32[128,4,128]{2,1,0:T(4,128)S(1)}, u32[]{:S(2)}, u32[]{:S(2)}) %collective-permute-start.2) | collective-permute-done | bytes 262176 | tf_op jit(solution)/shard_map/ppermute | solution.py:469
  45.6 2.0 %solve.1 = (f32[1,1,2,6]{3,2,1,0:T(2,128)}, f32[1,1,2,6]{3,2,1,0:T(2,128)}) custom-call(f32[512,128]{1,0:T(8,128)S(1)} %bitcast.5, f32[512,128]{1,0:T(8,128)S(1)} %bitcast.6), custom_call_target="tpu_custom_call" | custom-call | tf_op jit(solution)/shard_map/solve/pallas_call | solution.py:471
  (1 shorter events, 0.0 us)
Async XLA Ops:
  0.6 1.1 %copy-start = (bf16[1,1,2,5,64,512]{5,4,3,2,1,0:T(8,128)(2,1)S(1)}, bf16[1,1,2,5,64,512]{5,4,3,2,1,0:T(8,128)(2,1)}, u32[]{:S(2)}) copy-start(bf16[1,1,2,5,64,512]{5,4,3,2,1,0:T(8,128)(2,1)} %strips.5) | copy-start | bytes 1966084
  1.7 6.8 %copy-start.1 = (bf16[1,1,2,5,64,512]{5,4,3,2,1,0:T(8,128)(2,1)S(1)}, bf16[1,1,2,5,64,512]{5,4,3,2,1,0:T(8,128)(2,1)}, u32[]{:S(2)}) copy-start(bf16[1,1,2,5,64,512]{5,4,3,2,1,0:T(8,128)(2,1)} %strips.5) | copy-start | bytes 1966084
  2.1 6.5 %copy-start.2 = (s32[1,1,2,3,2]{3,4,2,1,0:T(2,128)S(1)}, s32[1,1,2,3,2]{3,4,2,1,0:T(2,128)}, u32[]{:S(2)}) copy-start(s32[1,1,2,3,2]{3,4,2,1,0:T(2,128)} %param.6) | copy-start | bytes 148
  2.1 8.9 %collective-permute-start = (bf16[2,64,512]{2,1,0:T(8,128)(2,1)S(1)}, bf16[2,64,512]{2,1,0:T(8,128)(2,1)S(1)}, u32[]{:S(2)}, u32[]{:S(2)}) collective-permute-start(bf16[2,64,512]{2,1,0:T(8,128)(2,1)S(1)} %get-tuple-element.6), channel_id=1, source_target_pairs={{1,0},{2,1},{3,2},{4,3},{5,4},{6,5},{7,6},{8,7},{9,8},{10,9},{11,1... | collective-permute-start | bytes 393224 | tf_op jit(solution)/shard_map/ppermute | solution.py:442
  3.4 5.2 %copy-start.3 = (s32[1,1,2,3]{3,2,1,0:T(2,128)S(1)}, s32[1,1,2,3]{3,2,1,0:T(2,128)}, u32[]{:S(2)}) copy-start(s32[1,1,2,3]{3,2,1,0:T(2,128)} %mask.1) | copy-start | bytes 76
  3.4 5.2 %copy-start.4 = (f32[1,1,2]{2,1,0:T(1,128)S(1)}, f32[1,1,2]{2,1,0:T(1,128)}, u32[]{:S(2)}) copy-start(f32[1,1,2]{2,1,0:T(1,128)} %stiff.1) | copy-start | bytes 28
  3.4 7.6 %collective-permute-start.1 = (bf16[2,64,512]{2,1,0:T(8,128)(2,1)S(1)}, bf16[2,64,512]{2,1,0:T(8,128)(2,1)S(1)}, u32[]{:S(2)}, u32[]{:S(2)}) collective-permute-start(bf16[2,64,512]{2,1,0:T(8,128)(2,1)S(1)} %get-tuple-element.7), channel_id=1, source_target_pairs={{32,0},{64,32},{96,64},{128,96},{160,128},{192,160},{224,192},{33,... | collective-permute-start | bytes 393224 | tf_op jit(solution)/shard_map/ppermute | solution.py:443
  41.4 4.1 %collective-permute-start.2 = (f32[128,4,128]{2,1,0:T(4,128)S(1)}, f32[128,4,128]{2,1,0:T(4,128)S(1)}, u32[]{:S(2)}, u32[]{:S(2)}) collective-permute-start(f32[128,4,128]{2,1,0:T(4,128)S(1)} %all_to_all.5), channel_id=1, source_target_pairs={{0,32},{32,0},{1,33},{33,1},{2,34},{34,2},{3,35},{35,3},{4,36},{36... | collective-permute-start | bytes 786440 | tf_op jit(solution)/shard_map/ppermute | solution.py:469

commit v2 on v1

v2 whole, which is shorter than its diff:
```python
import functools

import jax
import jax.numpy as jnp
from jax import lax
from jax.experimental import pallas as pl
from jax.experimental.pallas import tpu as pltpu
from jax.sharding import Mesh, PartitionSpec as P

ITERS = 3
H, W = 64, 512
F32 = jnp.float32
LANES = 128
RIGHT, CROSS, PULL, AGAIN = 24, (32, 40), (48, 56), 64
MOMENTS = 3 * W
ROWS = 2 * H + 8
SCALE = 2.0**-17

PACK_LIMIT = 2 << 20

VMEM = pl.BlockSpec(memory_space=pltpu.VMEM)
SMEM = pl.BlockSpec(memory_space=pltpu.SMEM)


def iota(shape, axis):
    return lax.broadcasted_iota(jnp.int32, shape, axis)


def store_gradients(image, gx_ref, gy_ref):
    col = iota((H, W), 1)
    row = iota((H, W), 0)
    ahead = jnp.where(col < W - 1, pltpu.roll(image, W - 1, 1), 0.0)
    behind = jnp.where(col > 0, pltpu.roll(image, 1, 1), 0.0)
    gx_ref[...] = ahead - behind
    below = jnp.where(row < H - 1, pltpu.roll(image, H - 1, 0), 0.0)
    above = jnp.where(row > 0, pltpu.roll(image, 1, 0), 0.0)
    gy_ref[...] = below - above


def row_moments(sums, level):
    s = iota((8, LANES), 0).astype(F32)
    c = 0.5 + s / H
    out = [sums[0], c * sums[0] - sums[1] * 0.125]
    if level == 3:
        out.append(c * c * sums[0] - (0.25 * c) * sums[1] + (2.0 * sums[2] - sums[1]) * (1.0 / 64.0))
    return out


def accumulate(fields, level):
    sums = None
    for k in range(8):
        values = fields(k)
        if sums is None:
            sums = [[v] * lv for v, lv in zip(values, level)]
            continue
        new = []
        for v, old, lv in zip(values, sums, level):
            now = [old[0] + v]
            for q in range(1, lv):
                now.append(old[q] + now[q - 1])
            new.append(now)
        sums = new
    return [row_moments(s, lv) for s, lv in zip(sums, level)]


def tree8(vs):
    s = iota((8, LANES), 0)
    m4 = s < 4
    w = []
    for i in range(4):
        x = jnp.where(m4, vs[i], vs[i + 4])
        y = jnp.where(m4, vs[i + 4], vs[i])
        w.append(x + pltpu.roll(y, 4, 0))
    m2 = (s & 2) == 0
    z = []
    for i in range(2):
        x = jnp.where(m2, w[i], w[i + 2])
        y = jnp.where(m2, w[i + 2], w[i])
        z.append(x + jnp.where(m2, pltpu.roll(y, 6, 0), pltpu.roll(y, 2, 0)))
    m1 = (s & 1) == 0
    x = jnp.where(m1, z[0], z[1])
    y = jnp.where(m1, z[1], z[0])
    return x + jnp.where(m1, pltpu.roll(y, 7, 0), pltpu.roll(y, 1, 0))


def put_group(group, lt, found, table):
    order = [found[(f, t)] for f in range(4) for t in range(2)]
    for q in range(3):
        vs = [v[q] if len(v) > q else None for v in order]
        rows = pl.ds(8 * group, 8), pl.ds(q * W + lt * LANES, LANES)
        if all(v is None for v in vs):
            table[rows] = jnp.zeros((8, LANES), F32)
        else:
            table[rows] = tree8([jnp.zeros((8, LANES), F32) if v is None else v for v in vs])


def column_moments(table, wide):
    r = iota((8, MOMENTS), 0)
    j = iota((8, MOMENTS), 1)
    u = (j & (W - 1)).astype(F32) / W - 0.5
    q = j // W
    one = ((r == 0) & (q == 0)) | ((r == 2) & (q == 1)) | ((r == 5) & (q == 2))
    first = ((r == 1) & (q == 0)) | ((r == 4) & (q == 1))
    weight = jnp.where(one, 1.0, jnp.where(first, u, jnp.where((r == 3) & (q == 0), u * u, 0.0))) * SCALE
    dims = (((1,), (1,)), ((), ()))
    wide[...] = jnp.zeros_like(wide)
    wide[:, 0 : table.shape[0]] = lax.dot_general(
        weight, table[...], dims, precision=lax.Precision.HIGHEST, preferred_element_type=F32
    )
    return wide[...]


def pair_fields(gxa, gya, gxb, gyb, misfit, lanes):
    def fields(k):
        rows = pl.ds(8 * k, 8)
        xa, ya, xb, yb, m = (ref[rows, lanes] for ref in (gxa, gya, gxb, gyb, misfit))
        return [xa * xb, xa * yb, ya * xb, ya * yb, xa * m, ya * m, xb * m, yb * m]

    return fields


def self_fields(gx, gy, lanes):
    def fields(k):
        rows = pl.ds(8 * k, 8)
        x, y = gx[rows, lanes], gy[rows, lanes]
        return [x * x, x * y, y * y]

    return fields


PAIR_LEVEL = (3, 3, 3, 3, 2, 2, 2, 2)


def by_tile(values, shape=(8, LANES)):
    return jnp.where((iota(shape, 1) & 1) == 0, values[0], values[1])


def in_range(lane, start, length):
    return (lane >= start) & (lane < start + length)


def own_exists(mask):
    down = lax.axis_index("tile") < 31
    sec = 2 * lax.axis_index("y") + lax.axis_index("core") < 7
    out = []
    for k, inside in ((1, down), (2, sec)):
        out.append([jnp.where((mask[0, 0, t, k] == 1) & inside, 1.0, 0.0) for t in range(2)])
    return out


def pack_kernel(strips, mask_in, offset_in, bottoms, patches, mask, offset, sems, small_sems):
    small = [pltpu.make_async_copy(mask_in, mask, small_sems.at[0]),
             pltpu.make_async_copy(offset_in, offset, small_sems.at[1])]
    for copy in small:
        copy.start()
    copies = []
    for n, (ref, image) in enumerate(((bottoms, 3), (patches, 4))):
        for t in range(2):
            copies.append(
                pltpu.make_async_copy(strips.at[0, 0, t, image], ref.at[pl.ds(H * t, H)], sems.at[2 * n + t])
            )
    for copy in copies:
        copy.start()
    for copy in small:
        copy.wait()
    exists = own_exists(mask)
    row = iota((8, W), 0)
    for n, ref in enumerate((bottoms, patches)):
        lines = [by_tile(exists[n], (8, W))]
        for d in range(2):
            lines.append(by_tile([offset[0, 0, t, d, n + 1].astype(F32) for t in range(2)], (8, W)))
        block = jnp.where(row == 0, lines[0], jnp.where(row == 1, lines[1], jnp.where(row == 2, lines[2], 0.0)))
        ref[2 * H :, :] = block.astype(jnp.bfloat16)
    for copy in copies:
        copy.wait()


def own_kernel(strips, mask, offset, stiff, out, facts, second, grad, misfit, table, wide):
    kinds = ((1, 0), (3, 3), (4, 4), (2, 2))
    refs = {}
    for kind, images in enumerate(kinds):
        for t in range(2):
            home = grad.at[kind, t] if kind < 2 else second.at[3 - kind, t]
            refs[(kind, t)] = (home.at[0], home.at[1])
            store_gradients(strips[0, 0, t, images[t]].astype(F32), *refs[(kind, t)])
    misfit[...] = strips[0, 0, 0, 1].astype(F32) - strips[0, 0, 1, 0].astype(F32)
    for lt in range(4):
        lanes = pl.ds(lt * LANES, LANES)
        found = {}
        for kind in range(4):
            for t in range(2):
                got = accumulate(self_fields(*refs[(kind, t)], lanes), (3, 3, 3))
                for n in range(3):
                    found[(3 * kind + n, t)] = got[n]
        for group in range(3):
            put_group(group, lt, {(f, t): found[(4 * group + f, t)] for f in range(4) for t in range(2)}, table)
        got = accumulate(pair_fields(*refs[(0, 0)], *refs[(0, 1)], misfit, lanes), PAIR_LEVEL)
        right = {(0, 0): got[0], (0, 1): got[1], (1, 0): got[2], (1, 1): got[3],
                 (2, 0): got[4], (3, 0): got[5], (2, 1): got[6], (3, 1): got[7]}
        put_group(3, lt, right, table)
    out[...] = column_moments(table, wide)
    row = iota((8, LANES), 0)
    lane = iota((8, LANES), 1)
    even = (lane & 1) == 0
    down, sec = own_exists(mask)
    right = jnp.where(mask[0, 0, 0, 0] == 1, 1.0, 0.0)
    pull = in_range(lane, RIGHT + 4, 4)
    factor = jnp.where(lane < 6, right, 0.0)
    factor = jnp.where(in_range(lane, 6, 6), by_tile(down), factor)
    factor = jnp.where(in_range(lane, 12, 6), by_tile(sec), factor)
    factor = jnp.where(in_range(lane, RIGHT, 4), -right, factor)
    factor = jnp.where(pull, jnp.where(even, -2.0, 2.0) * right, factor)
    shift = [offset[0, 0, 0, d, 0].astype(F32) for d in range(2)]
    moved = (~even) & ((lane < 6) | pull)
    lines = [factor]
    lines += [jnp.where(moved, shift[d], 0.0) for d in range(2)]
    lines += [by_tile([stiff[0, 0, t] for t in range(2)])]
    lines += [jnp.full((8, LANES), shift[d], F32) for d in range(2)]
    total = jnp.zeros((8, LANES), F32)
    for n, line in enumerate(lines):
        total = jnp.where(row == n, line, total)
    facts[...] = total


def pair_moments(kind, strips, sent, second, grad, misfit, table, wide):
    for t in range(2):
        a = sent[H * t : H * (t + 1), :].astype(F32)
        store_gradients(a, grad.at[t, 0], grad.at[t, 1])
        misfit[t] = a - strips[0, 0, t, (2, 4)[kind]].astype(F32)
    for lt in range(4):
        lanes = pl.ds(lt * LANES, LANES)
        cross, pull = {}, {}
        for t in range(2):
            g = [grad.at[t, 0], grad.at[t, 1], second.at[kind, t, 0], second.at[kind, t, 1]]
            got = accumulate(pair_fields(*g, misfit.at[t], lanes), PAIR_LEVEL)
            for n in range(4):
                cross[(n, t)] = got[n]
                pull[(n, t)] = got[4 + n]
        put_group(0, lt, cross, table)
        put_group(1, lt, pull, table)
    found = column_moments(table, wide)
    lane = iota((8, LANES), 1)
    moved = jnp.where(in_range(lane, PULL[kind], 8), pltpu.roll(found, PULL[kind] - 8, 1), 0.0)
    return jnp.where(in_range(lane, CROSS[kind], 8), pltpu.roll(found, CROSS[kind], 1), moved)


def down_kernel(strips, upper, second, own, out, grad, misfit, table, wide):
    out[...] = own[...] + pair_moments(0, strips, upper, second, grad, misfit, table, wide)


def sec_kernel(strips, upper, before, second, own, facts, out, grad, misfit, table, wide):
    moments = own[...] + pair_moments(1, strips, before, second, grad, misfit, table, wide)
    lane = iota((1, LANES), 1)
    wide_lane = iota((8, LANES), 1)
    moments = moments + jnp.where(in_range(wide_lane, AGAIN, 6), pltpu.roll(moments, AGAIN - 12, 1), 0.0)
    factor, au, av = facts[0:1, :], facts[1:2, :], facts[2:3, :]
    told = []
    for kind, sent in enumerate((upper, before)):
        known = sent[2 * H :, 0:LANES].astype(F32)
        exists, dx, dy = known[0:1], known[1:2], known[2:3]
        told += [dx, dy]
        alone = in_range(lane, (18, AGAIN)[kind], 6)
        pull_b = in_range(lane, PULL[kind] + 4, 4)
        factor = jnp.where(alone, exists, factor)
        factor = jnp.where(in_range(lane, CROSS[kind], 8), -exists, factor)
        factor = jnp.where(in_range(lane, PULL[kind], 4), -2.0 * exists, factor)
        factor = jnp.where(pull_b, 2.0 * exists, factor)
        au = jnp.where(alone | pull_b, dx, au)
        av = jnp.where(alone | pull_b, dy, av)
    au = au * (1.0 / W)
    av = av * (1.0 / H)
    one, u, v, uu, uv, vv = (moments[n : n + 1, :] for n in range(6))
    lines = [one, u + au * one, v + av * one, uu + 2.0 * au * u + au * au * one,
             uv + au * v + av * u + au * av * one, vv + 2.0 * av * v + av * av * one]
    row = iota((8, LANES), 0)
    full = jnp.zeros((8, LANES), F32)
    for n, line in enumerate(lines):
        full = jnp.where(row == n, line * factor, full)

    def back(x, by):
        return pltpu.roll(x, LANES - by, 1)

    alone = full + back(full, 6) + back(full, 12) + back(full, 18) + back(full, AGAIN)
    alone = pltpu.roll(alone, 58, 1)
    ends = in_range(wide_lane, 58, 2) | in_range(wide_lane, 62, 2)
    alone = jnp.where(ends & ((row == 0) | (row == 3) | (row == 5)), alone + facts[3:4, :], alone)
    load = full + back(full, 24) + back(full, 32)
    final = jnp.where(in_range(wide_lane, 28, 4), load, full)
    final = jnp.where(in_range(wide_lane, 52, 4), back(full, 4), final)
    final = jnp.where(in_range(wide_lane, 58, 6), alone, final)
    tail = (told, [facts[4:5, :], facts[5:6, :]])
    for r in range(2):
        line = jnp.zeros((1, LANES), F32)
        for n, value in enumerate(tail[r]):
            line = jnp.where(in_range(lane, 120 + 2 * n, 2), value, line)
        for n, move in ((2, 56), (1, 16), (0, 104)):
            part = pltpu.roll(final, move, 1)[3 * r + n : 3 * r + n + 1, :]
            line = jnp.where(in_range(lane, 40 * n, 40), part, line)
        out[r : r + 1, :] = line


def solve_kernel(mine, theirs, update_out, residual_out, table):
    core = lax.axis_index("core")
    place = lax.axis_index("y") * 32 + lax.axis_index("tile")
    sub = iota((8, LANES), 0)
    lane = iota((8, LANES), 1)
    c0 = (sub & 1) == 0
    t0 = (sub & 2) == 0
    live = sub < 4
    for r in range(2):
        a = mine[pl.ds(r, LANES, stride=2), :]
        b = theirs[pl.ds(r, LANES, stride=2), :]
        first = jnp.where(core == 0, a, b)
        second = jnp.where(core == 0, b, a)
        table[pl.ds(256 * r, LANES, stride=2), :] = first.T
        table[pl.ds(256 * r + 1, LANES, stride=2), :] = second.T

    def read(r, place):
        return table[pl.ds(256 * r + 4 * place, 8), :]

    def low3(place):
        return read(0, 20 + place), read(0, 40 + place), read(0, place)

    def all6(place):
        return (read(1, place), read(1, 20 + place), read(0, 20 + place), read(1, 40 + place),
                read(0, 40 + place), read(0, place))

    def swap_tile(x):
        return jnp.where(t0, pltpu.roll(x, 6, 0), pltpu.roll(x, 2, 0))

    def swap_core(x):
        return jnp.where(c0, pltpu.roll(x, 7, 0), pltpu.roll(x, 1, 0))

    def row_from_next(x):
        return pltpu.roll(x, LANES - 1, 1)

    def row_to_next(x):
        return pltpu.roll(x, 1, 1)

    def sec_from_next(x):
        x = swap_core(x)
        return jnp.where(c0, x, pltpu.roll(x, LANES - 32, 1))

    def sec_to_next(x):
        x = swap_core(x)
        return jnp.where(c0, pltpu.roll(x, 32, 1), x)

    zero = jnp.zeros((8, LANES), F32)
    du = [read(1, 60) * (1.0 / W), read(0, 60) * (1.0 / W), read(0, 62) * (1.0 / W)]
    dv = [read(1, 61) * (1.0 / H), read(0, 61) * (1.0 / H), read(0, 63) * (1.0 / H)]
    au = jnp.where(t0, zero, du[0])
    av = jnp.where(t0, zero, dv[0])
    bu = jnp.where(t0, du[0], zero)
    bv = jnp.where(t0, dv[0], zero)
    blocks = [all6(17 + n) for n in range(3)]
    square = ((0, 1, 2), (1, 3, 4), (2, 4, 5))
    diagonal = [[blocks[(i // 3) + (j // 3)][square[i % 3][j % 3]] for j in range(6)] for i in range(6)]

    lower = [[None] * 6 for _ in range(6)]
    scaled_col = [[None] * 6 for _ in range(6)]
    inverse_pivot = []
    work = {(i, j): diagonal[i][j] for i in range(6) for j in range(i + 1)}
    for j in range(6):
        inv = 1.0 / work[(j, j)]
        inverse_pivot.append(inv)
        for i in range(j + 1, 6):
            lower[i][j] = work[(i, j)] * inv
        for i in range(j + 1, 6):
            for k in range(j + 1, i + 1):
                work[(i, k)] = work[(i, k)] - lower[i][j] * work[(k, j)]
    inverse = [[None] * 6 for _ in range(6)]
    for j in range(6):
        for i in range(j + 1, 6):
            value = lower[i][j]
            for k in range(j + 1, i):
                value = value + lower[i][k] * inverse[k][j]
            inverse[i][j] = -value

    def precondition(v):
        mid = []
        for i in range(6):
            value = v[i]
            for j in range(i):
                value = value + inverse[i][j] * v[j]
            mid.append(value * inverse_pivot[i])
        out = []
        for i in range(6):
            value = mid[i]
            for j in range(i + 1, 6):
                value = value + inverse[j][i] * mid[j]
            out.append(value)
        return out

    def coupling(m, ra, rb, ca, cb):
        uu, uv, u, vv, v, one = m
        if ra is None:
            return [[uu + ca * u, uv + cb * u, u], [uv + ca * v, vv + cb * v, v], [u + ca * one, v + cb * one, one]]
        return [[uu + (ra + ca) * u, uv + ra * v + cb * u, u + ra * one],
                [uv + ca * v + rb * u, vv + (rb + cb) * v, v + rb * one],
                [u + ca * one, v + cb * one, one]]

    def join(xx, xy, yx, yy):
        return [a + b for a, b in zip(xx, xy)] + [a + b for a, b in zip(yx, yy)]

    down, across = (
        join(*(coupling(all6(place + i), None, None, du[n], dv[n]) for i in range(4))) for n, place in ((1, 4), (2, 8))
    )
    a6, b6 = all6(0), all6(1)
    sa6, sb6 = [swap_tile(x) for x in a6], [swap_tile(x) for x in b6]

    def pick(x, y):
        return [jnp.where(t0, p, q) for p, q in zip(x, y)]

    right = (pick(a6, sa6), pick(sa6, sb6), pick(b6, a6), pick(sb6, b6))
    right = join(*(coupling(m, au, av, bu, bv) for m in right))

    load = []
    for n in range(2):
        for x, y, z in zip(low3(2 + n), low3(12 + n), low3(14 + n)):
            load.append(x + row_from_next(y) + sec_from_next(z))

    def times(block, vector, transpose):
        out = []
        for i in range(6):
            value = None
            for j in range(6):
                term = (block[j][i] if transpose else block[i][j]) * vector[j]
                value = term if value is None else value + term
            out.append(value)
        return out

    def multiply(vector):
        parts = [times(diagonal, vector, False)]
        parts.append(times(right, [swap_tile(x) for x in vector], False))
        parts.append([row_from_next(x) for x in times(down, vector, False)])
        parts.append(times(down, [row_to_next(x) for x in vector], True))
        parts.append([sec_from_next(x) for x in times(across, vector, False)])
        parts.append(times(across, [sec_to_next(x) for x in vector], True))
        return [functools.reduce(jnp.add, line) for line in zip(*parts)]

    def inner(x, y):
        total = functools.reduce(jnp.add, [a * b for a, b in zip(x, y)])
        total = jnp.where(live, total, 0.0)
        return jnp.sum(total, axis=(0, 1), keepdims=True)

    residual = load
    direction = precondition(residual)
    rho = inner(residual, direction)
    update = None
    for step in range(ITERS):
        product = multiply(direction)
        size = rho / inner(direction, product)
        if update is None:
            update = [size * d for d in direction]
        else:
            update = [x + size * d for x, d in zip(update, direction)]
        residual = [r - size * p for r, p in zip(residual, product)]
        if step < ITERS - 1:
            scaled = precondition(residual)
            rho_next = inner(residual, scaled)
            ratio = rho_next / rho
            direction = [z + ratio * d for z, d in zip(scaled, direction)]
            rho = rho_next

    here = (lane == place) & live & ((sub & 1) == core)
    for vector, out in ((update, update_out), (residual, residual_out)):
        found = zero
        for i in range(6):
            value = jnp.sum(jnp.where(here, vector[i], 0.0), axis=1, keepdims=True)
            found = jnp.where(lane == i, value, found)
        found = found + pltpu.roll(found, 7, 0)
        out[0, 0, 0:1] = found[0:1, :6]
        out[0, 0, 1:2] = found[2:3, :6]


def shards(tile_strips, pair_mask, strip_offset, stiffness):
    tiles = lax.axis_size("tile")
    chips = lax.axis_size("y") * tiles
    sections = lax.axis_size("y") * 2
    offset = jnp.swapaxes(strip_offset, 3, 4)
    image = jax.ShapeDtypeStruct((ROWS, W), tile_strips.dtype)
    bottoms, patches = pl.pallas_call(
        pack_kernel,
        out_shape=(image, image),
        in_specs=[pl.BlockSpec(memory_space=pltpu.HBM)] * 3,
        out_specs=(VMEM, VMEM),
        scratch_shapes=[pltpu.SMEM(pair_mask.shape, jnp.int32), pltpu.SMEM(offset.shape, jnp.int32),
                        pltpu.SemaphoreType.DMA((4,)), pltpu.SemaphoreType.DMA((2,))],
        cost_estimate=pl.CostEstimate(flops=0, bytes_accessed=0, transcendentals=0),
        compiler_params=pltpu.CompilerParams(vmem_limit_bytes=PACK_LIMIT),
        name="pack",
    )(*(pltpu.with_memory_space_constraint(x, pltpu.HBM) for x in (tile_strips, pair_mask, offset)))
    upper = lax.ppermute(bottoms, "tile", [(i, i + 1) for i in range(tiles - 1)])
    before = lax.ppermute(patches, ("y", "core"), [(i, i + 1) for i in range(sections - 1)])
    small = jax.ShapeDtypeStruct((8, LANES), F32)
    wide = pltpu.VMEM((8, LANES), F32)
    params = pltpu.CompilerParams(vmem_limit_bytes=6 << 20)
    own, facts, second = pl.pallas_call(
        own_kernel,
        out_shape=(small, small, jax.ShapeDtypeStruct((2, 2, 2, H, W), F32)),
        in_specs=[VMEM, SMEM, SMEM, SMEM],
        out_specs=(VMEM, VMEM, VMEM),
        scratch_shapes=[pltpu.VMEM((2, 2, 2, H, W), F32), pltpu.VMEM((H, W), F32), pltpu.VMEM((32, MOMENTS), F32), wide],
        cost_estimate=pl.CostEstimate(flops=20_000_000, bytes_accessed=700_000, transcendentals=0),
        compiler_params=params,
        name="own_moments",
    )(tile_strips, pair_mask, offset, stiffness)
    scratch = [pltpu.VMEM((2, 2, H, W), F32), pltpu.VMEM((2, H, W), F32), pltpu.VMEM((16, MOMENTS), F32), wide]
    cost = pl.CostEstimate(flops=10_000_000, bytes_accessed=900_000, transcendentals=0)
    own = pl.pallas_call(
        down_kernel,
        out_shape=small,
        in_specs=[VMEM] * 4,
        out_specs=VMEM,
        scratch_shapes=scratch,
        cost_estimate=cost,
        compiler_params=params,
        name="down_moments",
    )(tile_strips, upper, second, own)
    message = pl.pallas_call(
        sec_kernel,
        out_shape=jax.ShapeDtypeStruct((2, LANES), F32),
        in_specs=[VMEM] * 6,
        out_specs=VMEM,
        scratch_shapes=scratch,
        cost_estimate=cost,
        compiler_params=params,
        name="sec_moments",
    )(tile_strips, upper, before, second, own, facts)
    sent = jnp.broadcast_to(message[None], (chips, 2, LANES))
    mine = lax.all_to_all(sent, ("y", "tile"), 0, 0)
    theirs = lax.ppermute(mine, "core", [(0, 1), (1, 0)])
    out = jax.ShapeDtypeStruct((1, 1, 2, 6), F32)
    outs = pl.pallas_call(
        solve_kernel,
        out_shape=(out, out),
        in_specs=[VMEM] * 2,
        out_specs=(VMEM, VMEM),
        scratch_shapes=[pltpu.VMEM((2 * 256 + 8, LANES), F32)],
        compiler_params=pltpu.CompilerParams(vmem_limit_bytes=4 << 20),
        name="solve",
    )(mine.reshape(chips * 2, LANES), theirs.reshape(chips * 2, LANES))
    return tuple(jnp.transpose(x, (3, 0, 1, 2)) for x in outs)


def solution(mesh):
    fine = Mesh(mesh.devices.reshape(4, 2, 32), ("y", "core", "tile"))
    sec = ("y", "core")
    return jax.shard_map(
        shards,
        mesh=fine,
        in_specs=(
            P(sec, "tile", None, None, None, None),
            P(sec, "tile", None, None),
            P(sec, "tile", None, None, None),
            P(sec, "tile", None),
        ),
        out_specs=(P(None, sec, "tile", None), P(None, sec, "tile", None)),
        check_vma=False,
    )
```

time: 47.7 us -> 45 us (0.943)
  blocking collectives: 28.7 us -> 25.7 us
  local copies, waits for them, and re-layouts: 1.17 us -> 0.07 us
  starting transfers between devices: 9.38 us -> 10.2 us
  Pallas kernels: 6.4 us -> 7.2 us
    all_to_all x1, blocking collectives: 28.7 us -> 25.7 us  [shards(): mine = lax.all_to_all(sent, ('y', 'tile'), 0, 0)]
    ppermute x2, starting transfers between devices: 6.4 us -> 8.12 us  [the longest x1 4.07 us: shards(): lax.ppermute(bottoms, 'tile', [(i, i + 1) for i in range(tiles - 1)])]
    unnamed x10 -> x8, local copies, waits for them, and re-layouts: 1.1 us -> 0.02 us
    ppermute x1, starting transfers between devices: 2.98 us -> 2.04 us  [shards(): theirs = lax.ppermute(mine, 'core', [(0, 1), (1, 0)])]
    pallas_call x3 -> x4, Pallas kernels: 4.44 us -> 5.37 us  [the longest x1 2.27 us: shards(): pl.pallas_call(own_kernel, out_shape=(small, small, jax.ShapeDtypeStruct(...]
  transfers between devices with their start and end apart: 3 -> 3, of which waited for: 1 -> 1; matrix products, arithmetic and copies ran while one was open for 0% -> 0% of each run, Pallas kernels for 5% -> 7%
where the time goes in v2:
time: 45 us; the launch traced here: 44.9 us
  blocking collectives  25.7 us (57%)
  starting transfers between devices  10.2 us (23%)
  Pallas kernels  7.2 us (16%)
  waiting for transfers between devices  0.99 us (2%)
  between operations  0.73 us (2%)
    all_to_all x1, blocking collectives, shards(): mine = lax.all_to_all(sent, ('y', 'tile'), 0, 0)  25.7 us
    ppermute x1, starting transfers between devices, shards(): lax.ppermute(bottoms, 'tile', [(i, i + 1) for i in range(tiles - 1)])  4.07 us
    ppermute x1, starting transfers between devices, shards(): lax.ppermute(patches, ('y', 'core'), [(i, i + 1) for i in range(sections...  4.05 us
    pallas_call x1, Pallas kernels, shards(): pl.pallas_call(own_kernel, out_shape=(small, small, jax.ShapeDtypeStruct(...  2.27 us
    ppermute x1, starting transfers between devices, shards(): theirs = lax.ppermute(mine, 'core', [(0, 1), (1, 0)])  2.04 us
    pallas_call x1, Pallas kernels, shards(): pl.pallas_call(solve_kernel, out_shape=(out, out), in_specs=[VMEM] * 2, o...  1.83 us
    pallas_call x1, Pallas kernels, shards(): pl.pallas_call(sec_kernel, out_shape=jax.ShapeDtypeStruct((2, LANES), F32...  1.21 us
    pallas_call x1, Pallas kernels, shards(): pl.pallas_call(pack_kernel, out_shape=(image, image), in_specs=[pl.BlockS...  1.05 us
  transfers between devices with their start and end apart: 3, of which 1 were waited for; matrix products, arithmetic and copies ran while one was open for 0% of the time, Pallas kernels for 7%

profile of v2, /device:TPU:1, one launch (start us, length us, event | category | flops | bytes accessed | tf_op | source)
XLA Modules:
  0.0 44.9 jit_solution(2435061378349155443)
XLA Ops:
  0.6 0.0 copy-start
  0.6 1.1 %pack.1 = (bf16[136,512]{1,0:T(8,128)(2,1)S(1)}, bf16[136,512]{1,0:T(8,128)(2,1)S(1)}) custom-call(bf16[1,1,2,5,64,512]{5,4,3,2,1,0:T(8,128)(2,1)} %strips.7, s32[1,1,2,3]{3,2,1,0:T(2,128)} %mask.1, s32[1,1,2,2,3]{4,3,2,1,0:T(2,128)} %bitcast.7), custom_call_target="tpu_custom_call" | custom-call | tf_op jit(solution)/shard_map/pack/pallas_call | solution.py:482
  1.7 0.0 copy-start.1
  1.7 0.0 copy-start.2
  1.7 0.0 copy-start.3
  1.7 4.1 %collective-permute-start = (bf16[136,512]{1,0:T(8,128)(2,1)S(1)}, bf16[136,512]{1,0:T(8,128)(2,1)S(1)}, u32[]{:S(2)}, u32[]{:S(2)}) collective-permute-start(bf16[136,512]{1,0:T(8,128)(2,1)S(1)} %get-tuple-element.9), channel_id=1, source_target_pairs={{0,1},{1,2},{2,3},{3,4},{4,5},{5,6},{6,7},{7,8},{8,9},{9,10},{10,1... | collective-permute-start | bytes 417800 | tf_op jit(solution)/shard_map/ppermute | solution.py:493
  5.8 4.0 %collective-permute-start.1 = (bf16[136,512]{1,0:T(8,128)(2,1)S(1)}, bf16[136,512]{1,0:T(8,128)(2,1)S(1)}, u32[]{:S(2)}, u32[]{:S(2)}) collective-permute-start(bf16[136,512]{1,0:T(8,128)(2,1)S(1)} %get-tuple-element.10), channel_id=1, source_target_pairs={{0,32},{32,64},{64,96},{96,128},{128,160},{160,192},{192,224},{1,3... | collective-permute-start | bytes 417800 | tf_op jit(solution)/shard_map/ppermute | solution.py:494
  9.9 0.0 copy-done
  9.9 0.0 copy-done.1
  9.9 0.0 copy-done.2
  9.9 0.0 copy-done.3
  9.9 2.3 %own_moments.1 = (f32[8,128]{1,0:T(8,128)S(1)}, f32[8,128]{1,0:T(8,128)S(1)}, f32[2,2,2,64,512]{4,3,2,1,0:T(8,128)S(1)}) custom-call(bf16[1,1,2,5,64,512]{5,4,3,2,1,0:T(8,128)(2,1)S(1)} %copy-done, s32[1,1,2,3]{3,2,1,0:T(2,128)S(1)} %copy-done.2, s32[1,1,2,2,3]{4,3,2,1,0:T(2,128)S(1)} %bitcast.8, f32[1,1,2]{2,1,0:T(1,128)S(1)} %copy-done.3), custom_call_target="tpu_custom_call" | custom-call | flops 20000000 | bytes 700000 | tf_op jit(solution)/shard_map/own_moments/pallas_call | solution.py:498
  12.2 0.0 collective-permute-done.upper
  12.2 0.8 %down_moments.1.own = f32[8,128]{1,0:T(8,128)S(1)} custom-call(bf16[1,1,2,5,64,512]{5,4,3,2,1,0:T(8,128)(2,1)S(1)} %copy-done, bf16[136,512]{1,0:T(8,128)(2,1)S(1)} %collective-permute-done.upper, f32[2,2,2,64,512]{4,3,2,1,0:T(8,128)S(1)} %get-tuple-element.11.second, f32[8,128]{1,0:T(8,128)S(1)} %get-tuple-element.12.own), custom_call_target="tpu_custom_call" | custom-call | flops 10000000 | bytes 900000 | tf_op jit(solution)/shard_map/down_moments/pallas_call | solution.py:510
  13.0 0.0 collective-permute-done.1.before
  13.0 1.2 %sec_moments.1 = f32[2,128]{1,0:T(2,128)S(1)} custom-call(bf16[1,1,2,5,64,512]{5,4,3,2,1,0:T(8,128)(2,1)S(1)} %copy-done, bf16[136,512]{1,0:T(8,128)(2,1)S(1)} %collective-permute-done.upper, bf16[136,512]{1,0:T(8,128)(2,1)S(1)} %collective-permute-done.1.before, f32[2,2,2,64,512]{4,3,2,1,0:T(8,128)S(1)} %get-tuple-element.11.second, ...), custom_call_target="tpu_custom_call" | custom-call | flops 10000000 | bytes 900000 | tf_op jit(solution)/shard_map/sec_moments/pallas_call | solution.py:520
  14.3 25.7 %all_to_all.5 = f32[128,2,128]{2,1,0:T(2,128)S(1)} all-to-all(f32[128,2,128]{2,1,0:T(2,128)S(1)} %broadcast_in_dim.2), channel_id=1, replica_groups=mesh['y'=4,'core'=2,'tile'=32] {'y','tile'}, dimensions={0} | all-to-all | bytes 262144 | tf_op jit(solution)/shard_map/all_to_all | solution.py:531
  40.0 2.0 %collective-permute-start.2 = (f32[128,2,128]{2,1,0:T(2,128)S(1)}, f32[128,2,128]{2,1,0:T(2,128)S(1)}, u32[]{:S(2)}, u32[]{:S(2)}) collective-permute-start(f32[128,2,128]{2,1,0:T(2,128)S(1)} %all_to_all.5), channel_id=1, source_target_pairs={{0,32},{32,0},{1,33},{33,1},{2,34},{34,2},{3,35},{35,3},{4,36},{36... | collective-permute-start | bytes 393224 | tf_op jit(solution)/shard_map/ppermute | solution.py:532
  42.0 1.0 %collective-permute-done.2 = f32[128,2,128]{2,1,0:T(2,128)S(1)} collective-permute-done((f32[128,2,128]{2,1,0:T(2,128)S(1)}, f32[128,2,128]{2,1,0:T(2,128)S(1)}, u32[]{:S(2)}, u32[]{:S(2)}) %collective-permute-start.2) | collective-permute-done | bytes 131104 | tf_op jit(solution)/shard_map/ppermute | solution.py:532
  43.0 1.8 %solve.1 = (f32[1,1,2,6]{3,2,1,0:T(2,128)}, f32[1,1,2,6]{3,2,1,0:T(2,128)}) custom-call(f32[256,128]{1,0:T(8,128)S(1)} %bitcast.5, f32[256,128]{1,0:T(8,128)S(1)} %bitcast.6), custom_call_target="tpu_custom_call" | custom-call | tf_op jit(solution)/shard_map/solve/pallas_call | solution.py:534
  (1 shorter events, 0.0 us)
Async XLA Ops:
  0.6 9.2 %copy-start = (bf16[1,1,2,5,64,512]{5,4,3,2,1,0:T(8,128)(2,1)S(1)}, bf16[1,1,2,5,64,512]{5,4,3,2,1,0:T(8,128)(2,1)}, u32[]{:S(2)}) copy-start(bf16[1,1,2,5,64,512]{5,4,3,2,1,0:T(8,128)(2,1)} %strips.7) | copy-start | bytes 1966084
  1.7 8.2 %copy-start.1 = (s32[1,1,2,3,2]{3,4,2,1,0:T(2,128)S(1)}, s32[1,1,2,3,2]{3,4,2,1,0:T(2,128)}, u32[]{:S(2)}) copy-start(s32[1,1,2,3,2]{3,4,2,1,0:T(2,128)} %param.6) | copy-start | bytes 148
  1.7 8.2 %copy-start.2 = (s32[1,1,2,3]{3,2,1,0:T(2,128)S(1)}, s32[1,1,2,3]{3,2,1,0:T(2,128)}, u32[]{:S(2)}) copy-start(s32[1,1,2,3]{3,2,1,0:T(2,128)} %mask.1) | copy-start | bytes 76
  1.7 8.2 %copy-start.3 = (f32[1,1,2]{2,1,0:T(1,128)S(1)}, f32[1,1,2]{2,1,0:T(1,128)}, u32[]{:S(2)}) copy-start(f32[1,1,2]{2,1,0:T(1,128)} %stiff.1) | copy-start | bytes 28
  1.7 10.4 %collective-permute-start = (bf16[136,512]{1,0:T(8,128)(2,1)S(1)}, bf16[136,512]{1,0:T(8,128)(2,1)S(1)}, u32[]{:S(2)}, u32[]{:S(2)}) collective-permute-start(bf16[136,512]{1,0:T(8,128)(2,1)S(1)} %get-tuple-element.9), channel_id=1, source_target_pairs={{0,1},{1,2},{2,3},{3,4},{4,5},{5,6},{6,7},{7,8},{8,9},{9,10},{10,1... | collective-permute-start | bytes 417800 | tf_op jit(solution)/shard_map/ppermute | solution.py:493
  5.8 7.2 %collective-permute-start.1 = (bf16[136,512]{1,0:T(8,128)(2,1)S(1)}, bf16[136,512]{1,0:T(8,128)(2,1)S(1)}, u32[]{:S(2)}, u32[]{:S(2)}) collective-permute-start(bf16[136,512]{1,0:T(8,128)(2,1)S(1)} %get-tuple-element.10), channel_id=1, source_target_pairs={{0,32},{32,64},{64,96},{96,128},{128,160},{160,192},{192,224},{1,3... | collective-permute-start | bytes 417800 | tf_op jit(solution)/shard_map/ppermute | solution.py:494
  40.0 3.0 %collective-permute-start.2 = (f32[128,2,128]{2,1,0:T(2,128)S(1)}, f32[128,2,128]{2,1,0:T(2,128)S(1)}, u32[]{:S(2)}, u32[]{:S(2)}) collective-permute-start(f32[128,2,128]{2,1,0:T(2,128)S(1)} %all_to_all.5), channel_id=1, source_target_pairs={{0,32},{32,0},{1,33},{33,1},{2,34},{34,2},{3,35},{35,3},{4,36},{36... | collective-permute-start | bytes 393224 | tf_op jit(solution)/shard_map/ppermute | solution.py:532

commit v3 on v2

--- a/solution.py
+++ b/solution.py
@@ -12,7 +12,6 @@
 F32 = jnp.float32
 LANES = 128
 RIGHT, CROSS, PULL, AGAIN = 24, (32, 40), (48, 56), 64
-MOMENTS = 3 * W
 ROWS = 2 * H + 8
 SCALE = 2.0**-17
 
@@ -26,23 +25,33 @@
     return lax.broadcasted_iota(jnp.int32, shape, axis)
 
 
-def store_gradients(image, gx_ref, gy_ref):
-    col = iota((H, W), 1)
-    row = iota((H, W), 0)
-    ahead = jnp.where(col < W - 1, pltpu.roll(image, W - 1, 1), 0.0)
-    behind = jnp.where(col > 0, pltpu.roll(image, 1, 1), 0.0)
-    gx_ref[...] = ahead - behind
-    below = jnp.where(row < H - 1, pltpu.roll(image, H - 1, 0), 0.0)
-    above = jnp.where(row > 0, pltpu.roll(image, 1, 0), 0.0)
-    gy_ref[...] = below - above
+def store_gradients(image, gx_ref, gy_ref, pad):
+    lane = iota((8, LANES), 1)
+    inner_first, inner_last = lane > 0, lane < LANES - 1
+    zero = jnp.zeros((8, LANES), F32)
+    tiles = []
+    for lt in range(4):
+        x = image(lt)
+        pad[lt, 0:8] = zero
+        pad[lt, 8 : 8 + H] = x
+        pad[lt, 8 + H : 16 + H] = zero
+        tiles.append([x[8 * k : 8 * k + 8] for k in range(8)])
+    for k in range(8):
+        ahead = [pltpu.roll(tiles[lt][k], LANES - 1, 1) for lt in range(4)] + [zero]
+        behind = [zero] + [pltpu.roll(tiles[lt][k], 1, 1) for lt in range(4)]
+        for lt in range(4):
+            here = pl.ds(8 * k, 8), pl.ds(lt * LANES, LANES)
+            gx_ref[here] = jnp.where(inner_last, ahead[lt], ahead[lt + 1]) - jnp.where(
+                inner_first, behind[lt + 1], behind[lt]
+            )
+            gy_ref[here] = pad[lt, 9 + 8 * k : 17 + 8 * k] - pad[lt, 7 + 8 * k : 15 + 8 * k]
 
 
 def row_moments(sums, level):
-    s = iota((8, LANES), 0).astype(F32)
-    c = 0.5 + s / H
+    c = 0.5 + iota((8, LANES), 0).astype(F32) / H
     out = [sums[0], c * sums[0] - sums[1] * 0.125]
     if level == 3:
-        out.append(c * c * sums[0] - (0.25 * c) * sums[1] + (2.0 * sums[2] - sums[1]) * (1.0 / 64.0))
+        out.append((c * c) * sums[0] - (0.25 * c + 1.0 / 64.0) * sums[1] + sums[2] * (1.0 / 32.0))
     return out
 
 
@@ -83,30 +92,33 @@
     return x + jnp.where(m1, pltpu.roll(y, 7, 0), pltpu.roll(y, 1, 0))
 
 
-def put_group(group, lt, found, table):
+def put_group(group, lt, found, total):
     order = [found[(f, t)] for f in range(4) for t in range(2)]
-    for q in range(3):
-        vs = [v[q] if len(v) > q else None for v in order]
-        rows = pl.ds(8 * group, 8), pl.ds(q * W + lt * LANES, LANES)
-        if all(v is None for v in vs):
-            table[rows] = jnp.zeros((8, LANES), F32)
-        else:
-            table[rows] = tree8([jnp.zeros((8, LANES), F32) if v is None else v for v in vs])
-
-
-def column_moments(table, wide):
-    r = iota((8, MOMENTS), 0)
-    j = iota((8, MOMENTS), 1)
-    u = (j & (W - 1)).astype(F32) / W - 0.5
-    q = j // W
-    one = ((r == 0) & (q == 0)) | ((r == 2) & (q == 1)) | ((r == 5) & (q == 2))
-    first = ((r == 1) & (q == 0)) | ((r == 4) & (q == 1))
-    weight = jnp.where(one, 1.0, jnp.where(first, u, jnp.where((r == 3) & (q == 0), u * u, 0.0))) * SCALE
+    low = [tree8([v[q] for v in order]) for q in range(2)]
+    u = (iota((8, LANES), 1) + lt * LANES).astype(F32) / W - 0.5
+    new = [low[0], u * low[0], low[1]]
+    if any(len(v) > 2 for v in order):
+        zero = jnp.zeros((8, LANES), F32)
+        new += [(u * u) * low[0], u * low[1], tree8([v[2] if len(v) > 2 else zero for v in order])]
+    for m, value in enumerate(new):
+        total[(m, group)] = total[(m, group)] + value if lt else value
+
+
+def column_moments(total, groups, table, wide):
     dims = (((1,), (1,)), ((), ()))
-    wide[...] = jnp.zeros_like(wide)
-    wide[:, 0 : table.shape[0]] = lax.dot_general(
-        weight, table[...], dims, precision=lax.Precision.HIGHEST, preferred_element_type=F32
-    )
+    zero = jnp.zeros((8, LANES), F32)
+    scale = jnp.full((8, LANES), SCALE, F32)
+    row = iota((8, 8 * groups), 0)
+    out = None
+    for m in range(6):
+        for group in range(groups):
+            table[m, pl.ds(8 * group, 8)] = total.get((m, group), zero)
+        part = lax.dot_general(
+            scale, table[m], dims, precision=lax.Precision.HIGHEST, preferred_element_type=F32
+        )
+        out = part if out is None else jnp.where(row == m, part, out)
+    wide[...] = zero
+    wide[0:6, 0 : 8 * groups] = out[0:6]
     return wide[...]
 
 
@@ -175,15 +187,18 @@
         copy.wait()
 
 
-def own_kernel(strips, mask, offset, stiff, out, facts, second, grad, misfit, table, wide):
+def own_kernel(strips, mask, offset, stiff, out, facts, second, grad, misfit, table, wide, pad):
     kinds = ((1, 0), (3, 3), (4, 4), (2, 2))
     refs = {}
     for kind, images in enumerate(kinds):
         for t in range(2):
             home = grad.at[kind, t] if kind < 2 else second.at[3 - kind, t]
             refs[(kind, t)] = (home.at[0], home.at[1])
-            store_gradients(strips[0, 0, t, images[t]].astype(F32), *refs[(kind, t)])
+            store_gradients(
+                lambda lt: strips[0, 0, t, images[t], :, lt * LANES : (lt + 1) * LANES].astype(F32), *refs[(kind, t)], pad
+            )
     misfit[...] = strips[0, 0, 0, 1].astype(F32) - strips[0, 0, 1, 0].astype(F32)
+    sums = {}
     for lt in range(4):
         lanes = pl.ds(lt * LANES, LANES)
         found = {}
@@ -193,12 +208,12 @@
                 for n in range(3):
                     found[(3 * kind + n, t)] = got[n]
         for group in range(3):
-            put_group(group, lt, {(f, t): found[(4 * group + f, t)] for f in range(4) for t in range(2)}, table)
+            put_group(group, lt, {(f, t): found[(4 * group + f, t)] for f in range(4) for t in range(2)}, sums)
         got = accumulate(pair_fields(*refs[(0, 0)], *refs[(0, 1)], misfit, lanes), PAIR_LEVEL)
         right = {(0, 0): got[0], (0, 1): got[1], (1, 0): got[2], (1, 1): got[3],
                  (2, 0): got[4], (3, 0): got[5], (2, 1): got[6], (3, 1): got[7]}
-        put_group(3, lt, right, table)
-    out[...] = column_moments(table, wide)
+        put_group(3, lt, right, sums)
+    out[...] = column_moments(sums, 4, table, wide)
     row = iota((8, LANES), 0)
     lane = iota((8, LANES), 1)
     even = (lane & 1) == 0
@@ -222,11 +237,14 @@
     facts[...] = total
 
 
-def pair_moments(kind, strips, sent, second, grad, misfit, table, wide):
+def pair_moments(kind, strips, sent, second, grad, misfit, table, wide, pad):
     for t in range(2):
-        a = sent[H * t : H * (t + 1), :].astype(F32)
-        store_gradients(a, grad.at[t, 0], grad.at[t, 1])
-        misfit[t] = a - strips[0, 0, t, (2, 4)[kind]].astype(F32)
+        rows = pl.ds(H * t, H)
+        store_gradients(
+            lambda lt: sent[rows, lt * LANES : (lt + 1) * LANES].astype(F32), grad.at[t, 0], grad.at[t, 1], pad
+        )
+        misfit[t] = sent[rows, :].astype(F32) - strips[0, 0, t, (2, 4)[kind]].astype(F32)
+    sums = {}
     for lt in range(4):
         lanes = pl.ds(lt * LANES, LANES)
         cross, pull = {}, {}
@@ -236,20 +254,20 @@
             for n in range(4):
                 cross[(n, t)] = got[n]
                 pull[(n, t)] = got[4 + n]
-        put_group(0, lt, cross, table)
-        put_group(1, lt, pull, table)
-    found = column_moments(table, wide)
+        put_group(0, lt, cross, sums)
+        put_group(1, lt, pull, sums)
+    found = column_moments(sums, 2, table, wide)
     lane = iota((8, LANES), 1)
     moved = jnp.where(in_range(lane, PULL[kind], 8), pltpu.roll(found, PULL[kind] - 8, 1), 0.0)
     return jnp.where(in_range(lane, CROSS[kind], 8), pltpu.roll(found, CROSS[kind], 1), moved)
 
 
-def down_kernel(strips, upper, second, own, out, grad, misfit, table, wide):
-    out[...] = own[...] + pair_moments(0, strips, upper, second, grad, misfit, table, wide)
-
-
-def sec_kernel(strips, upper, before, second, own, facts, out, grad, misfit, table, wide):
-    moments = own[...] + pair_moments(1, strips, before, second, grad, misfit, table, wide)
+def down_kernel(strips, upper, second, own, out, grad, misfit, table, wide, pad):
+    out[...] = own[...] + pair_moments(0, strips, upper, second, grad, misfit, table, wide, pad)
+
+
+def sec_kernel(strips, upper, before, second, own, facts, out, grad, misfit, table, wide, pad):
+    moments = own[...] + pair_moments(1, strips, before, second, grad, misfit, table, wide, pad)
     lane = iota((1, LANES), 1)
     wide_lane = iota((8, LANES), 1)
     moments = moments + jnp.where(in_range(wide_lane, AGAIN, 6), pltpu.roll(moments, AGAIN - 12, 1), 0.0)
@@ -429,13 +447,18 @@
             out.append(value)
         return out
 
+    down_next = [[row_from_next(x) for x in line] for line in down]
+    across_next = [[sec_from_next(x) for x in line] for line in across]
+
     def multiply(vector):
-        parts = [times(diagonal, vector, False)]
-        parts.append(times(right, [swap_tile(x) for x in vector], False))
-        parts.append([row_from_next(x) for x in times(down, vector, False)])
-        parts.append(times(down, [row_to_next(x) for x in vector], True))
-        parts.append([sec_from_next(x) for x in times(across, vector, False)])
-        parts.append(times(across, [sec_to_next(x) for x in vector], True))
+        parts = [
+            times(diagonal, vector, False),
+            times(right, [swap_tile(x) for x in vector], False),
+            times(down_next, [row_from_next(x) for x in vector], False),
+            times(down, [row_to_next(x) for x in vector], True),
+            times(across_next, [sec_from_next(x) for x in vector], False),
+            times(across, [sec_to_next(x) for x in vector], True),
+        ]
         return [functools.reduce(jnp.add, line) for line in zip(*parts)]
 
     def inner(x, y):
@@ -444,23 +467,22 @@
         return jnp.sum(total, axis=(0, 1), keepdims=True)
 
     residual = load
-    direction = precondition(residual)
-    rho = inner(residual, direction)
-    update = None
     for step in range(ITERS):
-        product = multiply(direction)
-        size = rho / inner(direction, product)
-        if update is None:
+        scaled = precondition(residual)
+        image = multiply(scaled)
+        rho_next, energy = inner(residual, scaled), inner(scaled, image)
+        if step == 0:
+            direction, product = scaled, image
+            size = rho_next / energy
             update = [size * d for d in direction]
         else:
+            ratio = rho_next / rho
+            size = rho_next / (energy - ratio * rho_next / size)
+            direction = [z + ratio * d for z, d in zip(scaled, direction)]
+            product = [z + ratio * d for z, d in zip(image, product)]
             update = [x + size * d for x, d in zip(update, direction)]
         residual = [r - size * p for r, p in zip(residual, product)]
-        if step < ITERS - 1:
-            scaled = precondition(residual)
-            rho_next = inner(residual, scaled)
-            ratio = rho_next / rho
-            direction = [z + ratio * d for z, d in zip(scaled, direction)]
-            rho = rho_next
+        rho = rho_next
 
     here = (lane == place) & live & ((sub & 1) == core)
     for vector, out in ((update, update_out), (residual, residual_out)):
@@ -490,22 +512,23 @@
         compiler_params=pltpu.CompilerParams(vmem_limit_bytes=PACK_LIMIT),
         name="pack",
     )(*(pltpu.with_memory_space_constraint(x, pltpu.HBM) for x in (tile_strips, pair_mask, offset)))
-    upper = lax.ppermute(bottoms, "tile", [(i, i + 1) for i in range(tiles - 1)])
-    before = lax.ppermute(patches, ("y", "core"), [(i, i + 1) for i in range(sections - 1)])
+    upper = lax.ppermute(bottoms, "tile", [(i, (i + 1) % tiles) for i in range(tiles)])
+    before = lax.ppermute(patches, ("y", "core"), [(i, (i + 1) % sections) for i in range(sections)])
     small = jax.ShapeDtypeStruct((8, LANES), F32)
     wide = pltpu.VMEM((8, LANES), F32)
+    pad = pltpu.VMEM((4, H + 16, LANES), F32)
     params = pltpu.CompilerParams(vmem_limit_bytes=6 << 20)
     own, facts, second = pl.pallas_call(
         own_kernel,
         out_shape=(small, small, jax.ShapeDtypeStruct((2, 2, 2, H, W), F32)),
         in_specs=[VMEM, SMEM, SMEM, SMEM],
         out_specs=(VMEM, VMEM, VMEM),
-        scratch_shapes=[pltpu.VMEM((2, 2, 2, H, W), F32), pltpu.VMEM((H, W), F32), pltpu.VMEM((32, MOMENTS), F32), wide],
+        scratch_shapes=[pltpu.VMEM((2, 2, 2, H, W), F32), pltpu.VMEM((H, W), F32), pltpu.VMEM((6, 32, LANES), F32), wide, pad],
         cost_estimate=pl.CostEstimate(flops=20_000_000, bytes_accessed=700_000, transcendentals=0),
         compiler_params=params,
         name="own_moments",
     )(tile_strips, pair_mask, offset, stiffness)
-    scratch = [pltpu.VMEM((2, 2, H, W), F32), pltpu.VMEM((2, H, W), F32), pltpu.VMEM((16, MOMENTS), F32), wide]
+    scratch = [pltpu.VMEM((2, 2, H, W), F32), pltpu.VMEM((2, H, W), F32), pltpu.VMEM((6, 16, LANES), F32), wide, pad]
     cost = pl.CostEstimate(flops=10_000_000, bytes_accessed=900_000, transcendentals=0)
     own = pl.pallas_call(
         down_kernel,

time: 45 us -> 42.1 us (0.936)
  waiting for transfers between devices: 0.99 us -> 6.57 us
  blocking collectives: 25.7 us -> 20.6 us
  starting transfers between devices: 10.2 us -> 7.2 us
    ppermute x2, waiting for transfers between devices: 0.01 us -> 5.58 us  [the longest x1 5.58 us: shards(): lax.ppermute(bottoms, 'tile', [(i, (i + 1) % tiles) for i in range(tiles)])]
    all_to_all x1, blocking collectives: 25.7 us -> 20.6 us  [shards(): mine = lax.all_to_all(sent, ('y', 'tile'), 0, 0)]
    ppermute x2, starting transfers between devices: 8.12 us -> 4.24 us  [the longest x1 2.14 us: shards(): lax.ppermute(patches, ('y', 'core'), [(i, (i + 1) % sections) for i in ra...]
    ppermute x1, starting transfers between devices: 2.04 us -> 2.96 us  [shards(): theirs = lax.ppermute(mine, 'core', [(0, 1), (1, 0)])]
  transfers between devices with their start and end apart: 3 -> 3, of which waited for: 1 -> 2; matrix products, arithmetic and copies ran while one was open for 0% -> 0% of each run, Pallas kernels for 7% -> 7%
where the time goes in v3:
time: 42.1 us; the launch traced here: 42 us
  blocking collectives  20.6 us (49%)
  starting transfers between devices  7.2 us (17%)
  Pallas kernels  6.86 us (16%)
  waiting for transfers between devices  6.57 us (16%)
  between operations  0.69 us (2%)
    all_to_all x1, blocking collectives, shards(): mine = lax.all_to_all(sent, ('y', 'tile'), 0, 0)  20.6 us
    ppermute x1, waiting for transfers between devices, shards(): lax.ppermute(bottoms, 'tile', [(i, (i + 1) % tiles) for i in range(tiles)])  5.58 us
    ppermute x1, starting transfers between devices, shards(): theirs = lax.ppermute(mine, 'core', [(0, 1), (1, 0)])  2.96 us
    pallas_call x1, Pallas kernels, shards(): pl.pallas_call(own_kernel, out_shape=(small, small, jax.ShapeDtypeStruct(...  2.2 us
    ppermute x1, starting transfers between devices, shards(): lax.ppermute(patches, ('y', 'core'), [(i, (i + 1) % sections) for i in ra...  2.14 us
    ppermute x1, starting transfers between devices, shards(): lax.ppermute(bottoms, 'tile', [(i, (i + 1) % tiles) for i in range(tiles)])  2.11 us
    pallas_call x1, Pallas kernels, shards(): pl.pallas_call(solve_kernel, out_shape=(out, out), in_specs=[VMEM] * 2, o...  1.63 us
    pallas_call x1, Pallas kernels, shards(): pl.pallas_call(sec_kernel, out_shape=jax.ShapeDtypeStruct((2, LANES), F32...  1.16 us
  transfers between devices with their start and end apart: 3, of which 2 were waited for; matrix products, arithmetic and copies ran while one was open for 0% of the time, Pallas kernels for 7%

profile of v3, /device:TPU:1, one launch (start us, length us, event | category | flops | bytes accessed | tf_op | source)
XLA Modules:
  0.0 42.0 jit_solution(9751437593044018608)
XLA Ops:
  0.6 0.0 copy-start
  0.6 1.1 %pack.1 = (bf16[136,512]{1,0:T(8,128)(2,1)S(1)}, bf16[136,512]{1,0:T(8,128)(2,1)S(1)}) custom-call(bf16[1,1,2,5,64,512]{5,4,3,2,1,0:T(8,128)(2,1)} %strips.7, s32[1,1,2,3]{3,2,1,0:T(2,128)} %mask.1, s32[1,1,2,2,3]{4,3,2,1,0:T(2,128)} %bitcast.7), custom_call_target="tpu_custom_call" | custom-call | tf_op jit(solution)/shard_map/pack/pallas_call | solution.py:504
  1.7 0.0 copy-start.1
  1.7 0.0 copy-start.2
  1.7 0.0 copy-start.3
  1.7 2.1 %collective-permute-start = (bf16[136,512]{1,0:T(8,128)(2,1)S(1)}, bf16[136,512]{1,0:T(8,128)(2,1)S(1)}, u32[]{:S(2)}, u32[]{:S(2)}) collective-permute-start(bf16[136,512]{1,0:T(8,128)(2,1)S(1)} %get-tuple-element.9), channel_id=1, source_target_pairs={{0,1},{1,2},{2,3},{3,4},{4,5},{5,6},{6,7},{7,8},{8,9},{9,10},{10,1... | collective-permute-start | bytes 417800 | tf_op jit(solution)/shard_map/ppermute | solution.py:515
  3.8 2.1 %collective-permute-start.1 = (bf16[136,512]{1,0:T(8,128)(2,1)S(1)}, bf16[136,512]{1,0:T(8,128)(2,1)S(1)}, u32[]{:S(2)}, u32[]{:S(2)}) collective-permute-start(bf16[136,512]{1,0:T(8,128)(2,1)S(1)} %get-tuple-element.10), channel_id=1, source_target_pairs={{0,32},{32,64},{64,96},{96,128},{128,160},{160,192},{192,224},{224... | collective-permute-start | bytes 417800 | tf_op jit(solution)/shard_map/ppermute | solution.py:516
  6.0 0.0 copy-done
  6.0 0.0 copy-done.1
  6.0 0.0 copy-done.2
  6.0 0.0 copy-done.3
  6.0 2.2 %own_moments.1 = (f32[8,128]{1,0:T(8,128)S(1)}, f32[8,128]{1,0:T(8,128)S(1)}, f32[2,2,2,64,512]{4,3,2,1,0:T(8,128)S(1)}) custom-call(bf16[1,1,2,5,64,512]{5,4,3,2,1,0:T(8,128)(2,1)S(1)} %copy-done, s32[1,1,2,3]{3,2,1,0:T(2,128)S(1)} %copy-done.2, s32[1,1,2,2,3]{4,3,2,1,0:T(2,128)S(1)} %bitcast.8, f32[1,1,2]{2,1,0:T(1,128)S(1)} %copy-done.3), custom_call_target="tpu_custom_call" | custom-call | flops 20000000 | bytes 700000 | tf_op jit(solution)/shard_map/own_moments/pallas_call | solution.py:521
  8.2 5.6 %collective-permute-done.upper = bf16[136,512]{1,0:T(8,128)(2,1)S(1)} collective-permute-done((bf16[136,512]{1,0:T(8,128)(2,1)S(1)}, bf16[136,512]{1,0:T(8,128)(2,1)S(1)}, u32[]{:S(2)}, u32[]{:S(2)}) %collective-permute-start) | collective-permute-done | bytes 139296 | tf_op jit(solution)/shard_map/ppermute | solution.py:515
  13.8 0.8 %down_moments.1.own = f32[8,128]{1,0:T(8,128)S(1)} custom-call(bf16[1,1,2,5,64,512]{5,4,3,2,1,0:T(8,128)(2,1)S(1)} %copy-done, bf16[136,512]{1,0:T(8,128)(2,1)S(1)} %collective-permute-done.upper, f32[2,2,2,64,512]{4,3,2,1,0:T(8,128)S(1)} %get-tuple-element.11.second, f32[8,128]{1,0:T(8,128)S(1)} %get-tuple-element.12.own), custom_call_target="tpu_custom_call" | custom-call | flops 10000000 | bytes 900000 | tf_op jit(solution)/shard_map/down_moments/pallas_call | solution.py:533
  14.6 0.0 collective-permute-done.1.before
  14.6 1.2 %sec_moments.1 = f32[2,128]{1,0:T(2,128)S(1)} custom-call(bf16[1,1,2,5,64,512]{5,4,3,2,1,0:T(8,128)(2,1)S(1)} %copy-done, bf16[136,512]{1,0:T(8,128)(2,1)S(1)} %collective-permute-done.upper, bf16[136,512]{1,0:T(8,128)(2,1)S(1)} %collective-permute-done.1.before, f32[2,2,2,64,512]{4,3,2,1,0:T(8,128)S(1)} %get-tuple-element.11.second, ...), custom_call_target="tpu_custom_call" | custom-call | flops 10000000 | bytes 900000 | tf_op jit(solution)/shard_map/sec_moments/pallas_call | solution.py:543
  15.8 20.6 %all_to_all.5 = f32[128,2,128]{2,1,0:T(2,128)S(1)} all-to-all(f32[128,2,128]{2,1,0:T(2,128)S(1)} %broadcast_in_dim.2), channel_id=1, replica_groups=mesh['y'=4,'core'=2,'tile'=32] {'y','tile'}, dimensions={0} | all-to-all | bytes 262144 | tf_op jit(solution)/shard_map/all_to_all | solution.py:554
  36.4 3.0 %collective-permute-start.2 = (f32[128,2,128]{2,1,0:T(2,128)S(1)}, f32[128,2,128]{2,1,0:T(2,128)S(1)}, u32[]{:S(2)}, u32[]{:S(2)}) collective-permute-start(f32[128,2,128]{2,1,0:T(2,128)S(1)} %all_to_all.5), channel_id=1, source_target_pairs={{0,32},{32,0},{1,33},{33,1},{2,34},{34,2},{3,35},{35,3},{4,36},{36... | collective-permute-start | bytes 393224 | tf_op jit(solution)/shard_map/ppermute | solution.py:555
  39.3 1.0 %collective-permute-done.2 = f32[128,2,128]{2,1,0:T(2,128)S(1)} collective-permute-done((f32[128,2,128]{2,1,0:T(2,128)S(1)}, f32[128,2,128]{2,1,0:T(2,128)S(1)}, u32[]{:S(2)}, u32[]{:S(2)}) %collective-permute-start.2) | collective-permute-done | bytes 131104 | tf_op jit(solution)/shard_map/ppermute | solution.py:555
  40.3 1.6 %solve.1 = (f32[1,1,2,6]{3,2,1,0:T(2,128)}, f32[1,1,2,6]{3,2,1,0:T(2,128)}) custom-call(f32[256,128]{1,0:T(8,128)S(1)} %bitcast.5, f32[256,128]{1,0:T(8,128)S(1)} %bitcast.6), custom_call_target="tpu_custom_call" | custom-call | tf_op jit(solution)/shard_map/solve/pallas_call | solution.py:557
  (1 shorter events, 0.0 us)
Async XLA Ops:
  0.6 5.4 %copy-start = (bf16[1,1,2,5,64,512]{5,4,3,2,1,0:T(8,128)(2,1)S(1)}, bf16[1,1,2,5,64,512]{5,4,3,2,1,0:T(8,128)(2,1)}, u32[]{:S(2)}) copy-start(bf16[1,1,2,5,64,512]{5,4,3,2,1,0:T(8,128)(2,1)} %strips.7) | copy-start | bytes 1966084
  1.7 4.3 %copy-start.1 = (s32[1,1,2,3,2]{3,4,2,1,0:T(2,128)S(1)}, s32[1,1,2,3,2]{3,4,2,1,0:T(2,128)}, u32[]{:S(2)}) copy-start(s32[1,1,2,3,2]{3,4,2,1,0:T(2,128)} %param.6) | copy-start | bytes 148
  1.7 4.3 %copy-start.2 = (s32[1,1,2,3]{3,2,1,0:T(2,128)S(1)}, s32[1,1,2,3]{3,2,1,0:T(2,128)}, u32[]{:S(2)}) copy-start(s32[1,1,2,3]{3,2,1,0:T(2,128)} %mask.1) | copy-start | bytes 76
  1.7 4.3 %copy-start.3 = (f32[1,1,2]{2,1,0:T(1,128)S(1)}, f32[1,1,2]{2,1,0:T(1,128)}, u32[]{:S(2)}) copy-start(f32[1,1,2]{2,1,0:T(1,128)} %stiff.1) | copy-start | bytes 28
  1.7 12.0 %collective-permute-start = (bf16[136,512]{1,0:T(8,128)(2,1)S(1)}, bf16[136,512]{1,0:T(8,128)(2,1)S(1)}, u32[]{:S(2)}, u32[]{:S(2)}) collective-permute-start(bf16[136,512]{1,0:T(8,128)(2,1)S(1)} %get-tuple-element.9), channel_id=1, source_target_pairs={{0,1},{1,2},{2,3},{3,4},{4,5},{5,6},{6,7},{7,8},{8,9},{9,10},{10,1... | collective-permute-start | bytes 417800 | tf_op jit(solution)/shard_map/ppermute | solution.py:515
  3.8 10.8 %collective-permute-start.1 = (bf16[136,512]{1,0:T(8,128)(2,1)S(1)}, bf16[136,512]{1,0:T(8,128)(2,1)S(1)}, u32[]{:S(2)}, u32[]{:S(2)}) collective-permute-start(bf16[136,512]{1,0:T(8,128)(2,1)S(1)} %get-tuple-element.10), channel_id=1, source_target_pairs={{0,32},{32,64},{64,96},{96,128},{128,160},{160,192},{192,224},{224... | collective-permute-start | bytes 417800 | tf_op jit(solution)/shard_map/ppermute | solution.py:516
  36.4 3.9 %collective-permute-start.2 = (f32[128,2,128]{2,1,0:T(2,128)S(1)}, f32[128,2,128]{2,1,0:T(2,128)S(1)}, u32[]{:S(2)}, u32[]{:S(2)}) collective-permute-start(f32[128,2,128]{2,1,0:T(2,128)S(1)} %all_to_all.5), channel_id=1, source_target_pairs={{0,32},{32,0},{1,33},{33,1},{2,34},{34,2},{3,35},{35,3},{4,36},{36... | collective-permute-start | bytes 393224 | tf_op jit(solution)/shard_map/ppermute | solution.py:555

commit v4 on v3

--- a/solution.py
+++ b/solution.py
@@ -6,6 +6,7 @@
 from jax.experimental import pallas as pl
 from jax.experimental.pallas import tpu as pltpu
 from jax.sharding import Mesh, PartitionSpec as P
+
 
 ITERS = 3
 H, W = 64, 512
@@ -237,7 +238,7 @@
     facts[...] = total
 
 
-def pair_moments(kind, strips, sent, second, grad, misfit, table, wide, pad):
+def pair_moments(kind, strips, sent, second, grad, misfit, pad):
     for t in range(2):
         rows = pl.ds(H * t, H)
         store_gradients(
@@ -256,18 +257,28 @@
                 pull[(n, t)] = got[4 + n]
         put_group(0, lt, cross, sums)
         put_group(1, lt, pull, sums)
-    found = column_moments(sums, 2, table, wide)
-    lane = iota((8, LANES), 1)
-    moved = jnp.where(in_range(lane, PULL[kind], 8), pltpu.roll(found, PULL[kind] - 8, 1), 0.0)
-    return jnp.where(in_range(lane, CROSS[kind], 8), pltpu.roll(found, CROSS[kind], 1), moved)
-
-
-def down_kernel(strips, upper, second, own, out, grad, misfit, table, wide, pad):
-    out[...] = own[...] + pair_moments(0, strips, upper, second, grad, misfit, table, wide, pad)
-
-
-def sec_kernel(strips, upper, before, second, own, facts, out, grad, misfit, table, wide, pad):
-    moments = own[...] + pair_moments(1, strips, before, second, grad, misfit, table, wide, pad)
+    return sums
+
+
+def sec_kernel(strips, before, second, out, grad, misfit, pad):
+    sums = pair_moments(1, strips, before, second, grad, misfit, pad)
+    for m in range(6):
+        for group in range(2):
+            out[m, pl.ds(8 * group, 8)] = sums.get((m, group), jnp.zeros((8, LANES), F32))
+
+
+def down_kernel(strips, upper, before, second, own, facts, sec, out, grad, misfit, pad, table, wide):
+    sums = pair_moments(0, strips, upper, second, grad, misfit, pad)
+    for m in range(6):
+        for group in range(2):
+            sums[(m, 2 + group)] = sec[m, pl.ds(8 * group, 8)]
+    found = column_moments(sums, 4, table, wide)
+    to = iota((8, LANES), 1)
+    moments = own[...] + jnp.where(
+        in_range(to, 40, 8),
+        pltpu.roll(found, 24, 1),
+        jnp.where(in_range(to, 48, 8), pltpu.roll(found, 40, 1), jnp.where(in_range(to, 32, 32), pltpu.roll(found, 32, 1), 0.0)),
+    )
     lane = iota((1, LANES), 1)
     wide_lane = iota((8, LANES), 1)
     moments = moments + jnp.where(in_range(wide_lane, AGAIN, 6), pltpu.roll(moments, AGAIN - 12, 1), 0.0)
@@ -375,7 +386,6 @@
     diagonal = [[blocks[(i // 3) + (j // 3)][square[i % 3][j % 3]] for j in range(6)] for i in range(6)]
 
     lower = [[None] * 6 for _ in range(6)]
-    scaled_col = [[None] * 6 for _ in range(6)]
     inverse_pivot = []
     work = {(i, j): diagonal[i][j] for i in range(6) for j in range(i + 1)}
     for j in range(6):
@@ -528,28 +538,28 @@
         compiler_params=params,
         name="own_moments",
     )(tile_strips, pair_mask, offset, stiffness)
-    scratch = [pltpu.VMEM((2, 2, H, W), F32), pltpu.VMEM((2, H, W), F32), pltpu.VMEM((6, 16, LANES), F32), wide, pad]
+    scratch = [pltpu.VMEM((2, 2, H, W), F32), pltpu.VMEM((2, H, W), F32), pad]
     cost = pl.CostEstimate(flops=10_000_000, bytes_accessed=900_000, transcendentals=0)
-    own = pl.pallas_call(
-        down_kernel,
-        out_shape=small,
-        in_specs=[VMEM] * 4,
-        out_specs=VMEM,
-        scratch_shapes=scratch,
-        cost_estimate=cost,
-        compiler_params=params,
-        name="down_moments",
-    )(tile_strips, upper, second, own)
-    message = pl.pallas_call(
+    sec = pl.pallas_call(
         sec_kernel,
-        out_shape=jax.ShapeDtypeStruct((2, LANES), F32),
-        in_specs=[VMEM] * 6,
+        out_shape=jax.ShapeDtypeStruct((6, 16, LANES), F32),
+        in_specs=[VMEM] * 3,
         out_specs=VMEM,
         scratch_shapes=scratch,
         cost_estimate=cost,
         compiler_params=params,
         name="sec_moments",
-    )(tile_strips, upper, before, second, own, facts)
+    )(tile_strips, before, second)
+    message = pl.pallas_call(
+        down_kernel,
+        out_shape=jax.ShapeDtypeStruct((2, LANES), F32),
+        in_specs=[VMEM] * 7,
+        out_specs=VMEM,
+        scratch_shapes=[*scratch, pltpu.VMEM((6, 32, LANES), F32), wide],
+        cost_estimate=cost,
+        compiler_params=params,
+        name="down_moments",
+    )(tile_strips, upper, before, second, own, facts, sec)
     sent = jnp.broadcast_to(message[None], (chips, 2, LANES))
     mine = lax.all_to_all(sent, ("y", "tile"), 0, 0)
     theirs = lax.ppermute(mine, "core", [(0, 1), (1, 0)])

time: 42.1 us -> 42.4 us (level)
  starting transfers between devices: 7.2 us -> 5.94 us
  waiting for transfers between devices: 6.57 us -> 7.81 us
  blocking collectives: 20.6 us -> 21.1 us
    ppermute x1, waiting for transfers between devices: 5.58 us -> 6.82 us  [shards(): lax.ppermute(bottoms, 'tile', [(i, (i + 1) % tiles) for i in range(tiles)])]
    ppermute x1, starting transfers between devices: 2.96 us -> 2.04 us  [shards(): theirs = lax.ppermute(mine, 'core', [(0, 1), (1, 0)])]
    ppermute x1, starting transfers between devices: 2.11 us -> 1.21 us  [shards(): lax.ppermute(bottoms, 'tile', [(i, (i + 1) % tiles) for i in range(tiles)])]
    all_to_all x1, blocking collectives: 20.6 us -> 21.1 us  [shards(): mine = lax.all_to_all(sent, ('y', 'tile'), 0, 0)]
    ppermute x1, starting transfers between devices: 2.14 us -> 2.69 us  [shards(): lax.ppermute(patches, ('y', 'core'), [(i, (i + 1) % sections) for i in ra...]
where the time goes in v4:
time: 42.4 us; the launch traced here: 42.2 us
  blocking collectives  21.1 us (50%)
  waiting for transfers between devices  7.81 us (18%)
  Pallas kernels  6.58 us (16%)
  starting transfers between devices  5.94 us (14%)
  between operations  0.69 us (2%)
    all_to_all x1, blocking collectives, shards(): mine = lax.all_to_all(sent, ('y', 'tile'), 0, 0)  21.1 us
    ppermute x1, waiting for transfers between devices, shards(): lax.ppermute(bottoms, 'tile', [(i, (i + 1) % tiles) for i in range(tiles)])  6.82 us
    ppermute x1, starting transfers between devices, shards(): lax.ppermute(patches, ('y', 'core'), [(i, (i + 1) % sections) for i in ra...  2.69 us
    pallas_call x1, Pallas kernels, shards(): pl.pallas_call(own_kernel, out_shape=(small, small, jax.ShapeDtypeStruct(...  2.2 us
    ppermute x1, starting transfers between devices, shards(): theirs = lax.ppermute(mine, 'core', [(0, 1), (1, 0)])  2.04 us
    pallas_call x1, Pallas kernels, shards(): pl.pallas_call(solve_kernel, out_shape=(out, out), in_specs=[VMEM] * 2, o...  1.63 us
    ppermute x1, starting transfers between devices, shards(): lax.ppermute(bottoms, 'tile', [(i, (i + 1) % tiles) for i in range(tiles)])  1.21 us
    pallas_call x1, Pallas kernels, shards(): pl.pallas_call(down_kernel, out_shape=jax.ShapeDtypeStruct((2, LANES), F3...  1.15 us
  transfers between devices with their start and end apart: 3, of which 2 were waited for; matrix products, arithmetic and copies ran while one was open for 0% of the time, Pallas kernels for 7%

profile of v4, /device:TPU:1, one launch (start us, length us, event | category | flops | bytes accessed | tf_op | source)
XLA Modules:
  0.0 42.2 jit_solution(12552898092860274141)
XLA Ops:
  0.6 0.0 copy-start
  0.6 1.1 %pack.1 = (bf16[136,512]{1,0:T(8,128)(2,1)S(1)}, bf16[136,512]{1,0:T(8,128)(2,1)S(1)}) custom-call(bf16[1,1,2,5,64,512]{5,4,3,2,1,0:T(8,128)(2,1)} %strips.7, s32[1,1,2,3]{3,2,1,0:T(2,128)} %mask.1, s32[1,1,2,2,3]{4,3,2,1,0:T(2,128)} %bitcast.7), custom_call_target="tpu_custom_call" | custom-call | tf_op jit(solution)/shard_map/pack/pallas_call | solution.py:514
  1.7 0.0 copy-start.1
  1.7 0.0 copy-start.2
  1.7 0.0 copy-start.3
  1.7 2.7 %collective-permute-start.1 = (bf16[136,512]{1,0:T(8,128)(2,1)S(1)}, bf16[136,512]{1,0:T(8,128)(2,1)S(1)}, u32[]{:S(2)}, u32[]{:S(2)}) collective-permute-start(bf16[136,512]{1,0:T(8,128)(2,1)S(1)} %get-tuple-element.10), channel_id=1, source_target_pairs={{0,32},{32,64},{64,96},{96,128},{128,160},{160,192},{192,224},{224... | collective-permute-start | bytes 417800 | tf_op jit(solution)/shard_map/ppermute | solution.py:526
  4.4 1.2 %collective-permute-start = (bf16[136,512]{1,0:T(8,128)(2,1)S(1)}, bf16[136,512]{1,0:T(8,128)(2,1)S(1)}, u32[]{:S(2)}, u32[]{:S(2)}) collective-permute-start(bf16[136,512]{1,0:T(8,128)(2,1)S(1)} %get-tuple-element.9), channel_id=1, source_target_pairs={{0,1},{1,2},{2,3},{3,4},{4,5},{5,6},{6,7},{7,8},{8,9},{9,10},{10,1... | collective-permute-start | bytes 417800 | tf_op jit(solution)/shard_map/ppermute | solution.py:525
  5.6 0.0 copy-done
  5.6 0.0 copy-done.1
  5.6 0.0 copy-done.2
  5.6 0.0 copy-done.3
  5.6 2.2 %own_moments.1 = (f32[8,128]{1,0:T(8,128)S(1)}, f32[8,128]{1,0:T(8,128)S(1)}, f32[2,2,2,64,512]{4,3,2,1,0:T(8,128)S(1)}) custom-call(bf16[1,1,2,5,64,512]{5,4,3,2,1,0:T(8,128)(2,1)S(1)} %copy-done, s32[1,1,2,3]{3,2,1,0:T(2,128)S(1)} %copy-done.2, s32[1,1,2,2,3]{4,3,2,1,0:T(2,128)S(1)} %bitcast.8, f32[1,1,2]{2,1,0:T(1,128)S(1)} %copy-done.3), custom_call_target="tpu_custom_call" | custom-call | flops 20000000 | bytes 700000 | tf_op jit(solution)/shard_map/own_moments/pallas_call | solution.py:531
  7.9 0.0 collective-permute-done.1.before
  7.9 0.5 %sec_moments.1.sec = f32[6,16,128]{2,1,0:T(8,128)S(1)} custom-call(bf16[1,1,2,5,64,512]{5,4,3,2,1,0:T(8,128)(2,1)S(1)} %copy-done, bf16[136,512]{1,0:T(8,128)(2,1)S(1)} %collective-permute-done.1.before, f32[2,2,2,64,512]{4,3,2,1,0:T(8,128)S(1)} %get-tuple-element.11.second), custom_call_target="tpu_custom_call" | custom-call | flops 10000000 | bytes 900000 | tf_op jit(solution)/shard_map/sec_moments/pallas_call | solution.py:543
  8.4 6.8 %collective-permute-done.upper = bf16[136,512]{1,0:T(8,128)(2,1)S(1)} collective-permute-done((bf16[136,512]{1,0:T(8,128)(2,1)S(1)}, bf16[136,512]{1,0:T(8,128)(2,1)S(1)}, u32[]{:S(2)}, u32[]{:S(2)}) %collective-permute-start) | collective-permute-done | bytes 139296 | tf_op jit(solution)/shard_map/ppermute | solution.py:525
  15.2 1.2 %down_moments.1 = f32[2,128]{1,0:T(2,128)S(1)} custom-call(bf16[1,1,2,5,64,512]{5,4,3,2,1,0:T(8,128)(2,1)S(1)} %copy-done, bf16[136,512]{1,0:T(8,128)(2,1)S(1)} %collective-permute-done.upper, bf16[136,512]{1,0:T(8,128)(2,1)S(1)} %collective-permute-done.1.before, f32[2,2,2,64,512]{4,3,2,1,0:T(8,128)S(1)} %get-tuple-element.11.second, ...), custom_call_target="tpu_custom_call" | custom-call | flops 10000000 | bytes 900000 | tf_op jit(solution)/shard_map/down_moments/pallas_call | solution.py:553
  16.4 21.1 %all_to_all.5 = f32[128,2,128]{2,1,0:T(2,128)S(1)} all-to-all(f32[128,2,128]{2,1,0:T(2,128)S(1)} %broadcast_in_dim.2), channel_id=1, replica_groups=mesh['y'=4,'core'=2,'tile'=32] {'y','tile'}, dimensions={0} | all-to-all | bytes 262144 | tf_op jit(solution)/shard_map/all_to_all | solution.py:564
  37.6 2.0 %collective-permute-start.2 = (f32[128,2,128]{2,1,0:T(2,128)S(1)}, f32[128,2,128]{2,1,0:T(2,128)S(1)}, u32[]{:S(2)}, u32[]{:S(2)}) collective-permute-start(f32[128,2,128]{2,1,0:T(2,128)S(1)} %all_to_all.5), channel_id=1, source_target_pairs={{0,32},{32,0},{1,33},{33,1},{2,34},{34,2},{3,35},{35,3},{4,36},{36... | collective-permute-start | bytes 393224 | tf_op jit(solution)/shard_map/ppermute | solution.py:565
  39.6 1.0 %collective-permute-done.2 = f32[128,2,128]{2,1,0:T(2,128)S(1)} collective-permute-done((f32[128,2,128]{2,1,0:T(2,128)S(1)}, f32[128,2,128]{2,1,0:T(2,128)S(1)}, u32[]{:S(2)}, u32[]{:S(2)}) %collective-permute-start.2) | collective-permute-done | bytes 131104 | tf_op jit(solution)/shard_map/ppermute | solution.py:565
  40.6 1.6 %solve.1 = (f32[1,1,2,6]{3,2,1,0:T(2,128)}, f32[1,1,2,6]{3,2,1,0:T(2,128)}) custom-call(f32[256,128]{1,0:T(8,128)S(1)} %bitcast.5, f32[256,128]{1,0:T(8,128)S(1)} %bitcast.6), custom_call_target="tpu_custom_call" | custom-call | tf_op jit(solution)/shard_map/solve/pallas_call | solution.py:567
  (1 shorter events, 0.0 us)
Async XLA Ops:
  0.6 5.0 %copy-start = (bf16[1,1,2,5,64,512]{5,4,3,2,1,0:T(8,128)(2,1)S(1)}, bf16[1,1,2,5,64,512]{5,4,3,2,1,0:T(8,128)(2,1)}, u32[]{:S(2)}) copy-start(bf16[1,1,2,5,64,512]{5,4,3,2,1,0:T(8,128)(2,1)} %strips.7) | copy-start | bytes 1966084
  1.7 3.9 %copy-start.1 = (s32[1,1,2,3,2]{3,4,2,1,0:T(2,128)S(1)}, s32[1,1,2,3,2]{3,4,2,1,0:T(2,128)}, u32[]{:S(2)}) copy-start(s32[1,1,2,3,2]{3,4,2,1,0:T(2,128)} %param.6) | copy-start | bytes 148
  1.7 3.9 %copy-start.2 = (s32[1,1,2,3]{3,2,1,0:T(2,128)S(1)}, s32[1,1,2,3]{3,2,1,0:T(2,128)}, u32[]{:S(2)}) copy-start(s32[1,1,2,3]{3,2,1,0:T(2,128)} %mask.1) | copy-start | bytes 76
  1.7 3.9 %copy-start.3 = (f32[1,1,2]{2,1,0:T(1,128)S(1)}, f32[1,1,2]{2,1,0:T(1,128)}, u32[]{:S(2)}) copy-start(f32[1,1,2]{2,1,0:T(1,128)} %stiff.1) | copy-start | bytes 28
  1.7 6.1 %collective-permute-start.1 = (bf16[136,512]{1,0:T(8,128)(2,1)S(1)}, bf16[136,512]{1,0:T(8,128)(2,1)S(1)}, u32[]{:S(2)}, u32[]{:S(2)}) collective-permute-start(bf16[136,512]{1,0:T(8,128)(2,1)S(1)} %get-tuple-element.10), channel_id=1, source_target_pairs={{0,32},{32,64},{64,96},{96,128},{128,160},{160,192},{192,224},{224... | collective-permute-start | bytes 417800 | tf_op jit(solution)/shard_map/ppermute | solution.py:526
  4.4 10.8 %collective-permute-start = (bf16[136,512]{1,0:T(8,128)(2,1)S(1)}, bf16[136,512]{1,0:T(8,128)(2,1)S(1)}, u32[]{:S(2)}, u32[]{:S(2)}) collective-permute-start(bf16[136,512]{1,0:T(8,128)(2,1)S(1)} %get-tuple-element.9), channel_id=1, source_target_pairs={{0,1},{1,2},{2,3},{3,4},{4,5},{5,6},{6,7},{7,8},{8,9},{9,10},{10,1... | collective-permute-start | bytes 417800 | tf_op jit(solution)/shard_map/ppermute | solution.py:525
  37.6 3.0 %collective-permute-start.2 = (f32[128,2,128]{2,1,0:T(2,128)S(1)}, f32[128,2,128]{2,1,0:T(2,128)S(1)}, u32[]{:S(2)}, u32[]{:S(2)}) collective-permute-start(f32[128,2,128]{2,1,0:T(2,128)S(1)} %all_to_all.5), channel_id=1, source_target_pairs={{0,32},{32,0},{1,33},{33,1},{2,34},{34,2},{3,35},{35,3},{4,36},{36... | collective-permute-start | bytes 393224 | tf_op jit(solution)/shard_map/ppermute | solution.py:565

commit v5 on v4

--- a/solution.py
+++ b/solution.py
@@ -105,7 +105,7 @@
         total[(m, group)] = total[(m, group)] + value if lt else value
 
 
-def column_moments(total, groups, table, wide):
+def column_moments(total, groups, table, wide, start=0):
     dims = (((1,), (1,)), ((), ()))
     zero = jnp.zeros((8, LANES), F32)
     scale = jnp.full((8, LANES), SCALE, F32)
@@ -119,7 +119,7 @@
         )
         out = part if out is None else jnp.where(row == m, part, out)
     wide[...] = zero
-    wide[0:6, 0 : 8 * groups] = out[0:6]
+    wide[0:6, start : start + 8 * groups] = out[0:6]
     return wide[...]
 
 
@@ -214,9 +214,10 @@
         right = {(0, 0): got[0], (0, 1): got[1], (1, 0): got[2], (1, 1): got[3],
                  (2, 0): got[4], (3, 0): got[5], (2, 1): got[6], (3, 1): got[7]}
         put_group(3, lt, right, sums)
-    out[...] = column_moments(sums, 4, table, wide)
+    found = column_moments(sums, 4, table, wide)
     row = iota((8, LANES), 0)
     lane = iota((8, LANES), 1)
+    out[...] = found + jnp.where(in_range(lane, AGAIN, 6), pltpu.roll(found, AGAIN - 12, 1), 0.0)
     even = (lane & 1) == 0
     down, sec = own_exists(mask)
     right = jnp.where(mask[0, 0, 0, 0] == 1, 1.0, 0.0)
@@ -270,18 +271,12 @@
 def down_kernel(strips, upper, before, second, own, facts, sec, out, grad, misfit, pad, table, wide):
     sums = pair_moments(0, strips, upper, second, grad, misfit, pad)
     for m in range(6):
-        for group in range(2):
-            sums[(m, 2 + group)] = sec[m, pl.ds(8 * group, 8)]
-    found = column_moments(sums, 4, table, wide)
-    to = iota((8, LANES), 1)
-    moments = own[...] + jnp.where(
-        in_range(to, 40, 8),
-        pltpu.roll(found, 24, 1),
-        jnp.where(in_range(to, 48, 8), pltpu.roll(found, 40, 1), jnp.where(in_range(to, 32, 32), pltpu.roll(found, 32, 1), 0.0)),
-    )
+        sums[(m, 2)] = sums.get((m, 1), jnp.zeros((8, LANES), F32))
+        sums[(m, 1)] = sec[m, 0:8]
+        sums[(m, 3)] = sec[m, 8:16]
+    moments = own[...] + column_moments(sums, 4, table, wide, CROSS[0])
     lane = iota((1, LANES), 1)
     wide_lane = iota((8, LANES), 1)
-    moments = moments + jnp.where(in_range(wide_lane, AGAIN, 6), pltpu.roll(moments, AGAIN - 12, 1), 0.0)
     factor, au, av = facts[0:1, :], facts[1:2, :], facts[2:3, :]
     told = []
     for kind, sent in enumerate((upper, before)):
@@ -309,8 +304,7 @@
     def back(x, by):
         return pltpu.roll(x, LANES - by, 1)
 
-    alone = full + back(full, 6) + back(full, 12) + back(full, 18) + back(full, AGAIN)
-    alone = pltpu.roll(alone, 58, 1)
+    alone = functools.reduce(jnp.add, [pltpu.roll(full, by, 1) for by in (58, 52, 46, 40, LANES + 58 - AGAIN)])
     ends = in_range(wide_lane, 58, 2) | in_range(wide_lane, 62, 2)
     alone = jnp.where(ends & ((row == 0) | (row == 3) | (row == 5)), alone + facts[3:4, :], alone)
     load = full + back(full, 24) + back(full, 32)

time: 42.4 us -> 42.2 us (level)
  no operation moved by 1% of the time
where the time goes in v5:
time: 42.2 us; the launch traced here: 42.1 us
  blocking collectives  21.1 us (50%)
  waiting for transfers between devices  7.71 us (18%)
  Pallas kernels  6.54 us (15%)
  starting transfers between devices  5.94 us (14%)
  between operations  0.69 us (2%)
    all_to_all x1, blocking collectives, shards(): mine = lax.all_to_all(sent, ('y', 'tile'), 0, 0)  21.1 us
    ppermute x1, waiting for transfers between devices, shards(): lax.ppermute(bottoms, 'tile', [(i, (i + 1) % tiles) for i in range(tiles)])  6.72 us
    ppermute x1, starting transfers between devices, shards(): lax.ppermute(patches, ('y', 'core'), [(i, (i + 1) % sections) for i in ra...  2.69 us
    pallas_call x1, Pallas kernels, shards(): pl.pallas_call(own_kernel, out_shape=(small, small, jax.ShapeDtypeStruct(...  2.3 us
    ppermute x1, starting transfers between devices, shards(): theirs = lax.ppermute(mine, 'core', [(0, 1), (1, 0)])  2.04 us
    pallas_call x1, Pallas kernels, shards(): pl.pallas_call(solve_kernel, out_shape=(out, out), in_specs=[VMEM] * 2, o...  1.63 us
    ppermute x1, starting transfers between devices, shards(): lax.ppermute(bottoms, 'tile', [(i, (i + 1) % tiles) for i in range(tiles)])  1.21 us
    pallas_call x1, Pallas kernels, shards(): pl.pallas_call(pack_kernel, out_shape=(image, image), in_specs=[pl.BlockS...  1.05 us
  transfers between devices with their start and end apart: 3, of which 2 were waited for; matrix products, arithmetic and copies ran while one was open for 0% of the time, Pallas kernels for 7%

profile of v5, /device:TPU:1, one launch (start us, length us, event | category | flops | bytes accessed | tf_op | source)
XLA Modules:
  0.0 42.1 jit_solution(15807748313985742215)
XLA Ops:
  0.6 0.0 copy-start
  0.6 1.1 %pack.1 = (bf16[136,512]{1,0:T(8,128)(2,1)S(1)}, bf16[136,512]{1,0:T(8,128)(2,1)S(1)}) custom-call(bf16[1,1,2,5,64,512]{5,4,3,2,1,0:T(8,128)(2,1)} %strips.7, s32[1,1,2,3]{3,2,1,0:T(2,128)} %mask.1, s32[1,1,2,2,3]{4,3,2,1,0:T(2,128)} %bitcast.7), custom_call_target="tpu_custom_call" | custom-call | tf_op jit(solution)/shard_map/pack/pallas_call | solution.py:508
  1.7 0.0 copy-start.1
  1.7 0.0 copy-start.2
  1.7 0.0 copy-start.3
  1.7 2.7 %collective-permute-start.1 = (bf16[136,512]{1,0:T(8,128)(2,1)S(1)}, bf16[136,512]{1,0:T(8,128)(2,1)S(1)}, u32[]{:S(2)}, u32[]{:S(2)}) collective-permute-start(bf16[136,512]{1,0:T(8,128)(2,1)S(1)} %get-tuple-element.10), channel_id=1, source_target_pairs={{0,32},{32,64},{64,96},{96,128},{128,160},{160,192},{192,224},{224... | collective-permute-start | bytes 417800 | tf_op jit(solution)/shard_map/ppermute | solution.py:520
  4.4 1.2 %collective-permute-start = (bf16[136,512]{1,0:T(8,128)(2,1)S(1)}, bf16[136,512]{1,0:T(8,128)(2,1)S(1)}, u32[]{:S(2)}, u32[]{:S(2)}) collective-permute-start(bf16[136,512]{1,0:T(8,128)(2,1)S(1)} %get-tuple-element.9), channel_id=1, source_target_pairs={{0,1},{1,2},{2,3},{3,4},{4,5},{5,6},{6,7},{7,8},{8,9},{9,10},{10,1... | collective-permute-start | bytes 417800 | tf_op jit(solution)/shard_map/ppermute | solution.py:519
  5.6 0.0 copy-done
  5.6 0.0 copy-done.1
  5.6 0.0 copy-done.2
  5.6 0.0 copy-done.3
  5.6 2.3 %own_moments.1 = (f32[8,128]{1,0:T(8,128)S(1)}, f32[8,128]{1,0:T(8,128)S(1)}, f32[2,2,2,64,512]{4,3,2,1,0:T(8,128)S(1)}) custom-call(bf16[1,1,2,5,64,512]{5,4,3,2,1,0:T(8,128)(2,1)S(1)} %copy-done, s32[1,1,2,3]{3,2,1,0:T(2,128)S(1)} %copy-done.2, s32[1,1,2,2,3]{4,3,2,1,0:T(2,128)S(1)} %bitcast.8, f32[1,1,2]{2,1,0:T(1,128)S(1)} %copy-done.3), custom_call_target="tpu_custom_call" | custom-call | flops 20000000 | bytes 700000 | tf_op jit(solution)/shard_map/own_moments/pallas_call | solution.py:525
  7.9 0.0 collective-permute-done.1.before
  8.0 0.5 %sec_moments.1.sec = f32[6,16,128]{2,1,0:T(8,128)S(1)} custom-call(bf16[1,1,2,5,64,512]{5,4,3,2,1,0:T(8,128)(2,1)S(1)} %copy-done, bf16[136,512]{1,0:T(8,128)(2,1)S(1)} %collective-permute-done.1.before, f32[2,2,2,64,512]{4,3,2,1,0:T(8,128)S(1)} %get-tuple-element.11.second), custom_call_target="tpu_custom_call" | custom-call | flops 10000000 | bytes 900000 | tf_op jit(solution)/shard_map/sec_moments/pallas_call | solution.py:537
  8.5 6.7 %collective-permute-done.upper = bf16[136,512]{1,0:T(8,128)(2,1)S(1)} collective-permute-done((bf16[136,512]{1,0:T(8,128)(2,1)S(1)}, bf16[136,512]{1,0:T(8,128)(2,1)S(1)}, u32[]{:S(2)}, u32[]{:S(2)}) %collective-permute-start) | collective-permute-done | bytes 139296 | tf_op jit(solution)/shard_map/ppermute | solution.py:519
  15.2 1.0 %down_moments.1 = f32[2,128]{1,0:T(2,128)S(1)} custom-call(bf16[1,1,2,5,64,512]{5,4,3,2,1,0:T(8,128)(2,1)S(1)} %copy-done, bf16[136,512]{1,0:T(8,128)(2,1)S(1)} %collective-permute-done.upper, bf16[136,512]{1,0:T(8,128)(2,1)S(1)} %collective-permute-done.1.before, f32[2,2,2,64,512]{4,3,2,1,0:T(8,128)S(1)} %get-tuple-element.11.second, ...), custom_call_target="tpu_custom_call" | custom-call | flops 10000000 | bytes 900000 | tf_op jit(solution)/shard_map/down_moments/pallas_call | solution.py:547
  16.3 21.1 %all_to_all.5 = f32[128,2,128]{2,1,0:T(2,128)S(1)} all-to-all(f32[128,2,128]{2,1,0:T(2,128)S(1)} %broadcast_in_dim.2), channel_id=1, replica_groups=mesh['y'=4,'core'=2,'tile'=32] {'y','tile'}, dimensions={0} | all-to-all | bytes 262144 | tf_op jit(solution)/shard_map/all_to_all | solution.py:558
  37.4 2.0 %collective-permute-start.2 = (f32[128,2,128]{2,1,0:T(2,128)S(1)}, f32[128,2,128]{2,1,0:T(2,128)S(1)}, u32[]{:S(2)}, u32[]{:S(2)}) collective-permute-start(f32[128,2,128]{2,1,0:T(2,128)S(1)} %all_to_all.5), channel_id=1, source_target_pairs={{0,32},{32,0},{1,33},{33,1},{2,34},{34,2},{3,35},{35,3},{4,36},{36... | collective-permute-start | bytes 393224 | tf_op jit(solution)/shard_map/ppermute | solution.py:559
  39.5 1.0 %collective-permute-done.2 = f32[128,2,128]{2,1,0:T(2,128)S(1)} collective-permute-done((f32[128,2,128]{2,1,0:T(2,128)S(1)}, f32[128,2,128]{2,1,0:T(2,128)S(1)}, u32[]{:S(2)}, u32[]{:S(2)}) %collective-permute-start.2) | collective-permute-done | bytes 131104 | tf_op jit(solution)/shard_map/ppermute | solution.py:559
  40.4 1.6 %solve.1 = (f32[1,1,2,6]{3,2,1,0:T(2,128)}, f32[1,1,2,6]{3,2,1,0:T(2,128)}) custom-call(f32[256,128]{1,0:T(8,128)S(1)} %bitcast.5, f32[256,128]{1,0:T(8,128)S(1)} %bitcast.6), custom_call_target="tpu_custom_call" | custom-call | tf_op jit(solution)/shard_map/solve/pallas_call | solution.py:561
  (1 shorter events, 0.0 us)
Async XLA Ops:
  0.6 5.0 %copy-start = (bf16[1,1,2,5,64,512]{5,4,3,2,1,0:T(8,128)(2,1)S(1)}, bf16[1,1,2,5,64,512]{5,4,3,2,1,0:T(8,128)(2,1)}, u32[]{:S(2)}) copy-start(bf16[1,1,2,5,64,512]{5,4,3,2,1,0:T(8,128)(2,1)} %strips.7) | copy-start | bytes 1966084
  1.7 3.9 %copy-start.1 = (s32[1,1,2,3,2]{3,4,2,1,0:T(2,128)S(1)}, s32[1,1,2,3,2]{3,4,2,1,0:T(2,128)}, u32[]{:S(2)}) copy-start(s32[1,1,2,3,2]{3,4,2,1,0:T(2,128)} %param.6) | copy-start | bytes 148
  1.7 3.9 %copy-start.2 = (s32[1,1,2,3]{3,2,1,0:T(2,128)S(1)}, s32[1,1,2,3]{3,2,1,0:T(2,128)}, u32[]{:S(2)}) copy-start(s32[1,1,2,3]{3,2,1,0:T(2,128)} %mask.1) | copy-start | bytes 76
  1.7 3.9 %copy-start.3 = (f32[1,1,2]{2,1,0:T(1,128)S(1)}, f32[1,1,2]{2,1,0:T(1,128)}, u32[]{:S(2)}) copy-start(f32[1,1,2]{2,1,0:T(1,128)} %stiff.1) | copy-start | bytes 28
  1.7 6.2 %collective-permute-start.1 = (bf16[136,512]{1,0:T(8,128)(2,1)S(1)}, bf16[136,512]{1,0:T(8,128)(2,1)S(1)}, u32[]{:S(2)}, u32[]{:S(2)}) collective-permute-start(bf16[136,512]{1,0:T(8,128)(2,1)S(1)} %get-tuple-element.10), channel_id=1, source_target_pairs={{0,32},{32,64},{64,96},{96,128},{128,160},{160,192},{192,224},{224... | collective-permute-start | bytes 417800 | tf_op jit(solution)/shard_map/ppermute | solution.py:520
  4.4 10.8 %collective-permute-start = (bf16[136,512]{1,0:T(8,128)(2,1)S(1)}, bf16[136,512]{1,0:T(8,128)(2,1)S(1)}, u32[]{:S(2)}, u32[]{:S(2)}) collective-permute-start(bf16[136,512]{1,0:T(8,128)(2,1)S(1)} %get-tuple-element.9), channel_id=1, source_target_pairs={{0,1},{1,2},{2,3},{3,4},{4,5},{5,6},{6,7},{7,8},{8,9},{9,10},{10,1... | collective-permute-start | bytes 417800 | tf_op jit(solution)/shard_map/ppermute | solution.py:519
  37.4 3.0 %collective-permute-start.2 = (f32[128,2,128]{2,1,0:T(2,128)S(1)}, f32[128,2,128]{2,1,0:T(2,128)S(1)}, u32[]{:S(2)}, u32[]{:S(2)}) collective-permute-start(f32[128,2,128]{2,1,0:T(2,128)S(1)} %all_to_all.5), channel_id=1, source_target_pairs={{0,32},{32,0},{1,33},{33,1},{2,34},{34,2},{3,35},{35,3},{4,36},{36... | collective-permute-start | bytes 393224 | tf_op jit(solution)/shard_map/ppermute | solution.py:559

commit v6 on v5

--- a/solution.py
+++ b/solution.py
@@ -333,10 +333,8 @@
     for r in range(2):
         a = mine[pl.ds(r, LANES, stride=2), :]
         b = theirs[pl.ds(r, LANES, stride=2), :]
-        first = jnp.where(core == 0, a, b)
-        second = jnp.where(core == 0, b, a)
-        table[pl.ds(256 * r, LANES, stride=2), :] = first.T
-        table[pl.ds(256 * r + 1, LANES, stride=2), :] = second.T
+        table[pl.ds(256 * r + core, LANES, stride=2), :] = a.T
+        table[pl.ds(256 * r + 1 - core, LANES, stride=2), :] = b.T
 
     def read(r, place):
         return table[pl.ds(256 * r + 4 * place, 8), :]

time: 42.2 us -> 42.3 us (level)
  no operation moved by 1% of the time
where the time goes in v6:
time: 42.3 us; the launch traced here: 42.1 us
  blocking collectives  21.1 us (50%)
  waiting for transfers between devices  7.71 us (18%)
  Pallas kernels  6.56 us (16%)
  starting transfers between devices  5.94 us (14%)
  between operations  0.69 us (2%)
    all_to_all x1, blocking collectives, shards(): mine = lax.all_to_all(sent, ('y', 'tile'), 0, 0)  21.1 us
    ppermute x1, waiting for transfers between devices, shards(): lax.ppermute(bottoms, 'tile', [(i, (i + 1) % tiles) for i in range(tiles)])  6.72 us
    ppermute x1, starting transfers between devices, shards(): lax.ppermute(patches, ('y', 'core'), [(i, (i + 1) % sections) for i in ra...  2.69 us
    pallas_call x1, Pallas kernels, shards(): pl.pallas_call(own_kernel, out_shape=(small, small, jax.ShapeDtypeStruct(...  2.3 us
    ppermute x1, starting transfers between devices, shards(): theirs = lax.ppermute(mine, 'core', [(0, 1), (1, 0)])  2.04 us
    pallas_call x1, Pallas kernels, shards(): pl.pallas_call(solve_kernel, out_shape=(out, out), in_specs=[VMEM] * 2, o...  1.65 us
    ppermute x1, starting transfers between devices, shards(): lax.ppermute(bottoms, 'tile', [(i, (i + 1) % tiles) for i in range(tiles)])  1.21 us
    pallas_call x1, Pallas kernels, shards(): pl.pallas_call(pack_kernel, out_shape=(image, image), in_specs=[pl.BlockS...  1.05 us
  transfers between devices with their start and end apart: 3, of which 2 were waited for; matrix products, arithmetic and copies ran while one was open for 0% of the time, Pallas kernels for 7%

profile of v6, /device:TPU:1, one launch (start us, length us, event | category | flops | bytes accessed | tf_op | source)
XLA Modules:
  0.0 42.1 jit_solution(363862241594878938)
XLA Ops:
  0.6 0.0 copy-start
  0.6 1.1 %pack.1 = (bf16[136,512]{1,0:T(8,128)(2,1)S(1)}, bf16[136,512]{1,0:T(8,128)(2,1)S(1)}) custom-call(bf16[1,1,2,5,64,512]{5,4,3,2,1,0:T(8,128)(2,1)} %strips.7, s32[1,1,2,3]{3,2,1,0:T(2,128)} %mask.1, s32[1,1,2,2,3]{4,3,2,1,0:T(2,128)} %bitcast.7), custom_call_target="tpu_custom_call" | custom-call | tf_op jit(solution)/shard_map/pack/pallas_call | solution.py:506
  1.7 0.0 copy-start.1
  1.7 0.0 copy-start.2
  1.7 0.0 copy-start.3
  1.7 2.7 %collective-permute-start.1 = (bf16[136,512]{1,0:T(8,128)(2,1)S(1)}, bf16[136,512]{1,0:T(8,128)(2,1)S(1)}, u32[]{:S(2)}, u32[]{:S(2)}) collective-permute-start(bf16[136,512]{1,0:T(8,128)(2,1)S(1)} %get-tuple-element.10), channel_id=1, source_target_pairs={{0,32},{32,64},{64,96},{96,128},{128,160},{160,192},{192,224},{224... | collective-permute-start | bytes 417800 | tf_op jit(solution)/shard_map/ppermute | solution.py:518
  4.4 1.2 %collective-permute-start = (bf16[136,512]{1,0:T(8,128)(2,1)S(1)}, bf16[136,512]{1,0:T(8,128)(2,1)S(1)}, u32[]{:S(2)}, u32[]{:S(2)}) collective-permute-start(bf16[136,512]{1,0:T(8,128)(2,1)S(1)} %get-tuple-element.9), channel_id=1, source_target_pairs={{0,1},{1,2},{2,3},{3,4},{4,5},{5,6},{6,7},{7,8},{8,9},{9,10},{10,1... | collective-permute-start | bytes 417800 | tf_op jit(solution)/shard_map/ppermute | solution.py:517
  5.6 0.0 copy-done
  5.6 0.0 copy-done.1
  5.6 0.0 copy-done.2
  5.6 0.0 copy-done.3
  5.6 2.3 %own_moments.1 = (f32[8,128]{1,0:T(8,128)S(1)}, f32[8,128]{1,0:T(8,128)S(1)}, f32[2,2,2,64,512]{4,3,2,1,0:T(8,128)S(1)}) custom-call(bf16[1,1,2,5,64,512]{5,4,3,2,1,0:T(8,128)(2,1)S(1)} %copy-done, s32[1,1,2,3]{3,2,1,0:T(2,128)S(1)} %copy-done.2, s32[1,1,2,2,3]{4,3,2,1,0:T(2,128)S(1)} %bitcast.8, f32[1,1,2]{2,1,0:T(1,128)S(1)} %copy-done.3), custom_call_target="tpu_custom_call" | custom-call | flops 20000000 | bytes 700000 | tf_op jit(solution)/shard_map/own_moments/pallas_call | solution.py:523
  7.9 0.0 collective-permute-done.1.before
  8.0 0.5 %sec_moments.1.sec = f32[6,16,128]{2,1,0:T(8,128)S(1)} custom-call(bf16[1,1,2,5,64,512]{5,4,3,2,1,0:T(8,128)(2,1)S(1)} %copy-done, bf16[136,512]{1,0:T(8,128)(2,1)S(1)} %collective-permute-done.1.before, f32[2,2,2,64,512]{4,3,2,1,0:T(8,128)S(1)} %get-tuple-element.11.second), custom_call_target="tpu_custom_call" | custom-call | flops 10000000 | bytes 900000 | tf_op jit(solution)/shard_map/sec_moments/pallas_call | solution.py:535
  8.5 6.7 %collective-permute-done.upper = bf16[136,512]{1,0:T(8,128)(2,1)S(1)} collective-permute-done((bf16[136,512]{1,0:T(8,128)(2,1)S(1)}, bf16[136,512]{1,0:T(8,128)(2,1)S(1)}, u32[]{:S(2)}, u32[]{:S(2)}) %collective-permute-start) | collective-permute-done | bytes 139296 | tf_op jit(solution)/shard_map/ppermute | solution.py:517
  15.2 1.0 %down_moments.1 = f32[2,128]{1,0:T(2,128)S(1)} custom-call(bf16[1,1,2,5,64,512]{5,4,3,2,1,0:T(8,128)(2,1)S(1)} %copy-done, bf16[136,512]{1,0:T(8,128)(2,1)S(1)} %collective-permute-done.upper, bf16[136,512]{1,0:T(8,128)(2,1)S(1)} %collective-permute-done.1.before, f32[2,2,2,64,512]{4,3,2,1,0:T(8,128)S(1)} %get-tuple-element.11.second, ...), custom_call_target="tpu_custom_call" | custom-call | flops 10000000 | bytes 900000 | tf_op jit(solution)/shard_map/down_moments/pallas_call | solution.py:545
  16.3 21.1 %all_to_all.5 = f32[128,2,128]{2,1,0:T(2,128)S(1)} all-to-all(f32[128,2,128]{2,1,0:T(2,128)S(1)} %broadcast_in_dim.2), channel_id=1, replica_groups=mesh['y'=4,'core'=2,'tile'=32] {'y','tile'}, dimensions={0} | all-to-all | bytes 262144 | tf_op jit(solution)/shard_map/all_to_all | solution.py:556
  37.4 2.0 %collective-permute-start.2 = (f32[128,2,128]{2,1,0:T(2,128)S(1)}, f32[128,2,128]{2,1,0:T(2,128)S(1)}, u32[]{:S(2)}, u32[]{:S(2)}) collective-permute-start(f32[128,2,128]{2,1,0:T(2,128)S(1)} %all_to_all.5), channel_id=1, source_target_pairs={{0,32},{32,0},{1,33},{33,1},{2,34},{34,2},{3,35},{35,3},{4,36},{36... | collective-permute-start | bytes 393224 | tf_op jit(solution)/shard_map/ppermute | solution.py:557
  39.5 1.0 %collective-permute-done.2 = f32[128,2,128]{2,1,0:T(2,128)S(1)} collective-permute-done((f32[128,2,128]{2,1,0:T(2,128)S(1)}, f32[128,2,128]{2,1,0:T(2,128)S(1)}, u32[]{:S(2)}, u32[]{:S(2)}) %collective-permute-start.2) | collective-permute-done | bytes 131104 | tf_op jit(solution)/shard_map/ppermute | solution.py:557
  40.4 1.7 %solve.1 = (f32[1,1,2,6]{3,2,1,0:T(2,128)}, f32[1,1,2,6]{3,2,1,0:T(2,128)}) custom-call(f32[256,128]{1,0:T(8,128)S(1)} %bitcast.5, f32[256,128]{1,0:T(8,128)S(1)} %bitcast.6), custom_call_target="tpu_custom_call" | custom-call | tf_op jit(solution)/shard_map/solve/pallas_call | solution.py:559
  (1 shorter events, 0.0 us)
Async XLA Ops:
  0.6 5.0 %copy-start = (bf16[1,1,2,5,64,512]{5,4,3,2,1,0:T(8,128)(2,1)S(1)}, bf16[1,1,2,5,64,512]{5,4,3,2,1,0:T(8,128)(2,1)}, u32[]{:S(2)}) copy-start(bf16[1,1,2,5,64,512]{5,4,3,2,1,0:T(8,128)(2,1)} %strips.7) | copy-start | bytes 1966084
  1.7 3.9 %copy-start.1 = (s32[1,1,2,3,2]{3,4,2,1,0:T(2,128)S(1)}, s32[1,1,2,3,2]{3,4,2,1,0:T(2,128)}, u32[]{:S(2)}) copy-start(s32[1,1,2,3,2]{3,4,2,1,0:T(2,128)} %param.6) | copy-start | bytes 148
  1.7 3.9 %copy-start.2 = (s32[1,1,2,3]{3,2,1,0:T(2,128)S(1)}, s32[1,1,2,3]{3,2,1,0:T(2,128)}, u32[]{:S(2)}) copy-start(s32[1,1,2,3]{3,2,1,0:T(2,128)} %mask.1) | copy-start | bytes 76
  1.7 3.9 %copy-start.3 = (f32[1,1,2]{2,1,0:T(1,128)S(1)}, f32[1,1,2]{2,1,0:T(1,128)}, u32[]{:S(2)}) copy-start(f32[1,1,2]{2,1,0:T(1,128)} %stiff.1) | copy-start | bytes 28
  1.7 6.2 %collective-permute-start.1 = (bf16[136,512]{1,0:T(8,128)(2,1)S(1)}, bf16[136,512]{1,0:T(8,128)(2,1)S(1)}, u32[]{:S(2)}, u32[]{:S(2)}) collective-permute-start(bf16[136,512]{1,0:T(8,128)(2,1)S(1)} %get-tuple-element.10), channel_id=1, source_target_pairs={{0,32},{32,64},{64,96},{96,128},{128,160},{160,192},{192,224},{224... | collective-permute-start | bytes 417800 | tf_op jit(solution)/shard_map/ppermute | solution.py:518
  4.4 10.8 %collective-permute-start = (bf16[136,512]{1,0:T(8,128)(2,1)S(1)}, bf16[136,512]{1,0:T(8,128)(2,1)S(1)}, u32[]{:S(2)}, u32[]{:S(2)}) collective-permute-start(bf16[136,512]{1,0:T(8,128)(2,1)S(1)} %get-tuple-element.9), channel_id=1, source_target_pairs={{0,1},{1,2},{2,3},{3,4},{4,5},{5,6},{6,7},{7,8},{8,9},{9,10},{10,1... | collective-permute-start | bytes 417800 | tf_op jit(solution)/shard_map/ppermute | solution.py:517
  37.4 3.0 %collective-permute-start.2 = (f32[128,2,128]{2,1,0:T(2,128)S(1)}, f32[128,2,128]{2,1,0:T(2,128)S(1)}, u32[]{:S(2)}, u32[]{:S(2)}) collective-permute-start(f32[128,2,128]{2,1,0:T(2,128)S(1)} %all_to_all.5), channel_id=1, source_target_pairs={{0,32},{32,0},{1,33},{33,1},{2,34},{34,2},{3,35},{35,3},{4,36},{36... | collective-permute-start | bytes 393224 | tf_op jit(solution)/shard_map/ppermute | solution.py:557
